TPU v7x, 32 devices: a whole 2x2x4 slice. The times are simulated.
32 devices in a mesh: section: 2 (over core), dp: 4 (over z), tensor: 4 (over y, x).
Axes of the slice: x: 2, y: 2, z: 4, core: 2. Of those that a mesh axis runs over, the one named last changes fastest.
Arguments:
- block_input: bfloat16 [2, 8, 1024, 768], P('section', 'dp', 'tensor'), may hold values from -6 to 6
- w_self: bfloat16 [2, 768, 3, 768], P('section', 'dp', None, 'tensor'), may hold values from -0.21875 to 0.21875
- w_self_out: bfloat16 [2, 768, 768], P('section', 'tensor', 'dp'), may hold values from -3 to 3
- w_cross: bfloat16 [2, 768, 2, 768], P('section', 'dp', None, 'tensor')
- w_up: bfloat16 [2, 768, 3072], P('section', 'dp', 'tensor'), may hold values from -0.21875 to 0.21875
- w_down: bfloat16 [2, 3072, 768], P('section', 'tensor', 'dp'), may hold values from -0.109375 to 0.109375
- norm_gains: bfloat16 [2, 3, 768], P('section'), may hold values from 0.5 to 1.5
- lengths: int32 [2, 8], P(None, 'dp'), may hold values from 128 to 1024, as said below
- task_mask: int32 [8, 1024], P('dp'), may hold values from 0 to 1, as said below
- out_grad: bfloat16 [8, 1024, 768], P('dp', 'tensor'), may hold values from -6 to 6
Outputs:
- block_output: bfloat16 [2, 8, 1024, 768], P('section', 'dp', 'tensor')
- input_grad: float32 [2, 8, 1024, 768], P('section', 'dp', 'tensor')
- w_self_grad: float32 [2, 768, 3, 768], P('section', 'dp', None, 'tensor')
- w_self_out_grad: float32 [2, 768, 768], P('section', 'tensor', 'dp')
- w_cross_grad: float32 [2, 768, 2, 768], P('section', 'dp', None, 'tensor')
- w_up_grad: float32 [2, 768, 3072], P('section', 'dp', 'tensor')
- w_down_grad: float32 [2, 3072, 768], P('section', 'tensor', 'dp')
- gains_grad: float32 [2, 2, 768], P('section')
- last_gain_grad: float32 [2, 768], P('section')
Inputs may be any that keep to these rules, and one draw needn't show every extreme that they name: Row 0 holds encoder lengths and row 1 decoder lengths; the first sequence has length 1024 in both rows. `task_mask`: position 0 of every sequence is 1.
All inputs are finite; a program needn't handle non-finite values.
Results may differ from a plain program's by a relative error of at most 0.02.
Values may be sent and summed in bfloat16 or wider, within the bound.
A program may use at most 320 MiB of HBM per device.

v0:
```python
import functools

import jax
import jax.numpy as jnp
from jax import lax
from jax.experimental import pallas as pl
from jax.experimental.pallas import tpu as pltpu
from jax.sharding import PartitionSpec as P

HEAD = 64
TILE = 128
EPSILON = 1e-05
SCORE_SCALE = 0.125
NEG_FILL = -1000000000.0
AXES = ("section", "dp", "tensor")
LOW = jnp.bfloat16
WIDE = jnp.float32


class Layout:
    def __init__(self):
        self.cores = lax.axis_size("section")
        self.planes = lax.axis_size("dp")
        self.chips = lax.axis_size("tensor")
        self.core = lax.axis_index("section")
        self.plane = lax.axis_index("dp")
        self.chip = lax.axis_index("tensor")
        self.role = self.chip % 2
        self.item = self.chip // 2
        self.is_decoder = self.role == 1
        self.relays = self.core == self.item

    def route(self, value, target):
        pairs = []
        for core in range(self.cores):
            for plane in range(self.planes):
                for chip in range(self.chips):
                    to = target(core, plane, chip)
                    if to is None:
                        continue
                    source = (core * self.planes + plane) * self.chips + chip
                    goal = (to[0] * self.planes + to[1]) * self.chips + to[2]
                    pairs.append((source, goal))
        return lax.ppermute(value, AXES, pairs)

    def other_core(self, value):
        return self.route(value, lambda c, z, t: (1 - c, z, t))


def normalize(values):
    centred = values - jnp.mean(values, axis=-1, keepdims=True)
    spread = jnp.mean(centred * centred, axis=-1, keepdims=True)
    scale = lax.rsqrt(spread + EPSILON)
    return centred * scale, scale


def layer_norm(values, gain):
    return normalize(values)[0] * gain


def norm_back(values, gain, grad):
    normal, scale = normalize(values)
    scaled = grad * gain
    first = jnp.mean(scaled, axis=-1, keepdims=True)
    second = jnp.mean(scaled * normal, axis=-1, keepdims=True)
    return (scaled - first - normal * second) * scale, jnp.sum(grad * normal, axis=0)


ORDER = (("q", 0), ("q", 1), ("q", 2), ("o", 2), ("o", 0), ("o", 1), ("k", 0), ("k", 1), ("v", 0), ("v", 1), ("k", 2), ("v", 2))


def pack_heads(parts):
    return jnp.concatenate([parts[n][:, HEAD * h : HEAD * (h + 1)] for n, h in ORDER], axis=1)


def unpack_heads(block, name):
    where = {(n, h): i for i, (n, h) in enumerate(ORDER)}
    return jnp.concatenate(
        [block[:, HEAD * where[(name, h)] : HEAD * (where[(name, h)] + 1)] for h in range(3)], axis=1
    )


def mm(left, right):
    return jnp.dot(left, right, preferred_element_type=WIDE)


def mm_nt(left, right):
    return lax.dot_general(left, right, (((1,), (1,)), ((), ())), preferred_element_type=WIDE)


def mm_tn(left, right):
    return lax.dot_general(left, right, (((0,), (0,)), ((), ())), preferred_element_type=WIDE)


def split_heads(value):
    return value.reshape(value.shape[0], -1, HEAD)


def attend(q, k, v, allowed):
    scores = jnp.einsum("qhd,khd->hqk", split_heads(q), split_heads(k), preferred_element_type=WIDE) * SCORE_SCALE
    scores = jnp.where(allowed[None], scores, NEG_FILL)
    top = jnp.max(scores, axis=-1, keepdims=True)
    power = jnp.exp(scores - top)
    total = jnp.sum(power, axis=-1, keepdims=True)
    probs = (power / total).astype(LOW)
    out = jnp.einsum("hqk,khd->qhd", probs, split_heads(v), preferred_element_type=WIDE)
    return out.astype(LOW).reshape(q.shape), top + jnp.log(total)


def attend_back(q, k, v, log_sum, d_out, allowed):
    scores = jnp.einsum("qhd,khd->hqk", split_heads(q), split_heads(k), preferred_element_type=WIDE) * SCORE_SCALE
    scores = jnp.where(allowed[None], scores, NEG_FILL)
    probs = jnp.exp(scores - log_sum)
    d_probs = jnp.einsum("qhd,khd->hqk", split_heads(d_out), split_heads(v), preferred_element_type=WIDE)
    inner = jnp.sum(probs * d_probs, axis=-1, keepdims=True)
    d_scores = (probs * (d_probs - inner)).astype(LOW)
    d_v = jnp.einsum("hqk,qhd->khd", probs.astype(LOW), split_heads(d_out), preferred_element_type=WIDE)
    d_q = jnp.einsum("hqk,khd->qhd", d_scores, split_heads(k), preferred_element_type=WIDE) * SCORE_SCALE
    d_k = jnp.einsum("hqk,qhd->khd", d_scores, split_heads(q), preferred_element_type=WIDE) * SCORE_SCALE
    return tuple(g.astype(LOW).reshape(q.shape) for g in (d_q, d_k, d_v))


def gelu_parts(value):
    coef = 0.7978845608028654
    cube = 0.044715
    inner = coef * (value + cube * value * value * value)
    soft = jnp.tanh(inner)
    slope = 0.5 * (1.0 + soft) + 0.5 * value * (1.0 - soft * soft) * coef * (1.0 + 3.0 * cube * value * value)
    return 0.5 * value * (1.0 + soft), slope


MESH = pl.DeviceIdType.MESH
GROUPS = ("att", "crs", "up", "dn")
BLOCK = 256
VMEM_BYTES = 62 * 2**20


def lanes(shape):
    return lax.broadcasted_iota(jnp.int32, shape, len(shape) - 1)


def subs(shape):
    return lax.broadcasted_iota(jnp.int32, shape, 0)


def strip(i, size):
    return pl.ds(pl.multiple_of(i * size, size), size)


def head_place(h):
    two = (h == 2).astype(jnp.int32)
    one = (h >= 1).astype(jnp.int32)
    return two, 2 + 2 * two, 3 + two, 1 - two, HEAD * (one - two), HEAD * one


def each(count, step, name=None):
    def run(i, carry):
        step(i)
        return carry

    with jax.named_scope(name or step.__name__):
        lax.fori_loop(0, count, run, 0)


class Place:
    def __init__(self, planes):
        self.planes = planes
        self.c = lax.axis_index("section")
        self.z = lax.axis_index("dp")
        self.t = lax.axis_index("tensor")
        self.y = lax.div(self.t, 2)
        self.r = lax.rem(self.t, 2)
        self.twin = (1 - self.c, self.z, self.t)
        self.above = (self.c, lax.rem(self.z + 1, planes), self.t)
        self.below = (self.c, lax.rem(self.z + planes - 1, planes), self.t)
        self.across = (self.c, self.z, lax.rem(self.t + 2, 4))
        self.beside = (self.c, self.z, self.t + 1 - 2 * self.r)
        self.relays = self.c == self.y
        self.encodes = self.r == 0
        self.decodes = self.r == 1

    def meet(self):
        barrier = pltpu.get_barrier_semaphore()
        peers = [self.above, self.below]
        for dc in range(2):
            for dt in range(4):
                if dc or dt:
                    peers.append((lax.rem(self.c + dc, 2), self.z, lax.rem(self.t + dt, 4)))
        for peer in peers:
            pl.semaphore_signal(barrier, inc=1, device_id=peer, device_id_type=MESH)
        pl.semaphore_wait(barrier, len(peers))


def push(source, goal, sent, got, device):
    return pltpu.make_async_remote_copy(
        src_ref=source, dst_ref=goal, send_sem=sent, recv_sem=got, device_id=device, device_id_type=MESH
    )


def both(first, second):
    return jnp.logical_and(first, second)


def center(values):
    middle = values - jnp.mean(values, axis=-1, keepdims=True)
    scale = lax.rsqrt(jnp.mean(middle * middle, axis=-1, keepdims=True) + EPSILON)
    return middle * scale, scale


def attend_block(h, p, o, lse, lse_row, bias, kx, qx, vt, causal):
    count = p.shape[0]
    qt, kt, vtile, ot, qlo, vlo = head_place(h)
    lane = lanes((count, TILE))
    in_q = both(lane >= qlo, lane < qlo + HEAD)
    in_v = both(lane >= vlo, lane < vlo + HEAD)
    spare = HEAD - qlo
    kx[...] = jnp.where(lane == spare, bias[...], jnp.where(in_q, p[:, strip(kt, TILE)], jnp.zeros((), LOW)))
    vt[...] = jnp.where(in_v, p[:, strip(vtile, TILE)].astype(WIDE), 1.0).T.astype(LOW)
    qx[...] = jnp.where(
        in_q, p[:, strip(qt, TILE)].astype(WIDE) * SCORE_SCALE, jnp.where(lane == spare, 1.0, 0.0)
    ).astype(LOW)
    size = count // 2 if causal else count

    def queries(i):
        q = strip(i, size) if causal else pl.ds(0, count)
        scores = mm_nt(kx[...], qx[q, :])
        if causal:
            scores = jnp.where(subs(scores.shape) <= lanes(scores.shape) + i * size, scores, NEG_FILL)
        top = jnp.max(scores, axis=0, keepdims=True)
        power = jnp.exp(scores - top).astype(LOW)
        out = mm(vt[...], power)
        total = jnp.where(vlo == 0, out[HEAD : HEAD + 1, :], out[0:1, :])
        result = (out / total).T
        lane = lanes((size, TILE))
        in_v = both(lane >= vlo, lane < vlo + HEAD)
        o[q, strip(ot, TILE)] = jnp.where(in_v, result, o[q, strip(ot, TILE)].astype(WIDE)).astype(LOW)
        row = subs((8, size))
        lse[:, q] = jnp.where(row == lse_row, top + jnp.log(total), lse[:, q])

    if causal:
        each(count // size, queries)
    else:
        queries(0)


SUMS = ("ffn", "crs", "att")
DIRECT = ("att", "up")
ASIDE = (("up", 0), ("dn", 0))


def split_three(value):
    high = value.astype(LOW).astype(WIDE)
    middle = (value - high).astype(LOW).astype(WIDE)
    return high, middle, value - high - middle


def attend_back_block(h, p, o, d_o, d_p, lse, lse_row, bias, kx, qx, vx, gx, kt_v, dk_v, dv_v, causal):
    count = p.shape[0]
    qt, kt, vtile, ot, qlo, vlo = head_place(h)
    lane = lanes((count, TILE))
    in_q = both(lane >= qlo, lane < qlo + HEAD)
    in_v = both(lane >= vlo, lane < vlo + HEAD)
    sq, sv = HEAD - qlo, HEAD - vlo
    keys = jnp.where(
        in_q, p[:, strip(kt, TILE)].astype(WIDE), jnp.where(both(lane > sq, lane < sq + 4), 1.0, 0.0)
    )
    keys = jnp.where(lane == sq, bias[...].astype(WIDE), keys)
    kx[...] = keys.astype(LOW)
    kt_v[...] = keys.T.astype(LOW)
    vx[...] = jnp.where(
        in_v, p[:, strip(vtile, TILE)].astype(WIDE), jnp.where(both(lane >= sv, lane < sv + 3), 1.0, 0.0)
    ).astype(LOW)
    own = jnp.sum(jnp.where(subs((8, count)) == lse_row, lse[...], 0.0), axis=0, keepdims=True)
    a, b, c = split_three(-jnp.broadcast_to(own, (TILE, count)).T)
    extra = jnp.where(
        lane == sq,
        1.0,
        jnp.where(lane == sq + 1, a, jnp.where(lane == sq + 2, b, jnp.where(lane == sq + 3, c, 0.0))),
    )
    qx[...] = jnp.where(in_q, p[:, strip(qt, TILE)].astype(WIDE) * SCORE_SCALE, extra).astype(LOW)
    grad = jnp.where(in_v, d_o[:, strip(ot, TILE)].astype(WIDE), 0.0)
    inner = jnp.sum(grad * o[:, strip(ot, TILE)].astype(WIDE), axis=-1, keepdims=True)
    a, b, c = split_three(-inner)
    gx[...] = (
        grad + jnp.where(lane == sv, a, jnp.where(lane == sv + 1, b, jnp.where(lane == sv + 2, c, 0.0)))
    ).astype(LOW)
    size = count // 2 if causal else count

    def place(q, tile_index, low, value):
        cut = strip(tile_index, TILE)
        lane = lanes(value.shape)
        inside = both(lane >= low, lane < low + HEAD)
        d_p[q, cut] = jnp.where(inside, value, d_p[q, cut].astype(WIDE)).astype(LOW)

    whole = pl.ds(0, count)
    if causal:
        dk_v[...] = jnp.zeros_like(dk_v)
        dv_v[...] = jnp.zeros_like(dv_v)

    def queries(i):
        q = strip(i, size) if causal else pl.ds(0, count)
        scores = mm_nt(kx[...], qx[q, :])
        if causal:
            scores = jnp.where(subs(scores.shape) <= lanes(scores.shape) + i * size, scores, NEG_FILL)
        probs = jnp.exp(scores)
        d_scores = (probs * mm_nt(vx[...], gx[q, :])).astype(LOW)
        d_v = mm(probs.astype(LOW), gx[q, :])
        d_k = mm(d_scores, qx[q, :])
        place(q, qt, qlo, mm(kt_v[...], d_scores).T * SCORE_SCALE)
        if causal:
            dk_v[...] += d_k
            dv_v[...] += d_v
        else:
            place(whole, kt, qlo, d_k)
            place(whole, vtile, vlo, d_v)

    if not causal:
        queries(0)
    else:
        each(count // size, queries)
        place(whole, kt, qlo, dk_v[...])
        place(whole, vtile, vlo, dv_v[...])


def block_kernel(
    planes, self_in, crs_in, up_in, dn_in, x_in, cot_in, gain_in, lengths, task_mask,
    block_out, grad_low, home_ffn, home_crs, home_att, gain_out,
    cot, first_k, x_k, second_k, late_k, memory_k, p_k, o_k, lse_k, pc_k, oc_k, lsec_k, act_k, grad_k, y3_k,
    dw_ffn, dw_crs, dw_att, yb_ffn, yb_crs, yb_att, zb_ffn, zb_crs, zb_att,
    att_v, crs_v, up_v, dn_v, a_v, b_v, o_v, do_v, mid_v, late_v, s_v, g_v, c_v, ta, tb, tc,
    send_v, recv_v, kx, qx, vx, gx, dk_v, dv_v, kt_v, lse_v, gain_v, gain_in_v, gain_buf, out_st, dw_st, sum_st,
    bias_self, bias_cross,
    x_sem, x_sent, y0_sent, c_sem, zw_got, zw_sent, yw_got, yw_sent, side_got, side_sent,
    row_got, row_sent, fwd_sem, cot_got, gain_sem, copy_sem, ex_got, ex_sent, mem_got, mem_sent, mf_got, mf_sent,
    dm_got, dm_sent, df_got, df_sent, y_got, y_sent, z_got, z_sent, home_got, home_sent,
    blk_got, blk_sent, gr_got, gr_sent, gr_hop_got, gr_hop_sent, sum_sem, dw_sem,
):
    at = Place(planes)
    c, z, t, y, r = at.c, at.z, at.t, at.y, at.r
    rows = x_in.shape[1]
    slot = s_v.shape[0]
    tiles = slot // BLOCK
    depth = up_in.shape[0]
    side = crs_in.shape[1]
    relay = at.relays
    other = jnp.logical_not(relay)
    vmem = {"att": att_v, "crs": crs_v, "up": up_v, "dn": dn_v}
    shard = {"att": self_in, "up": up_in, "dn": dn_in}
    here = pl.ds(pl.multiple_of(z * depth, depth), depth)
    dw = {"ffn": dw_ffn, "crs": dw_crs, "att": dw_att}
    yb = {"ffn": yb_ffn, "crs": yb_crs, "att": yb_att}
    zb = {"ffn": zb_ffn, "crs": zb_crs, "att": zb_att}
    home = {"ffn": home_ffn, "crs": home_crs, "att": home_att}
    names = {}

    def copying(name, source, goal):
        index = names.setdefault(name, len(names))
        return pltpu.make_async_copy(source, goal, copy_sem.at[index])

    def half_of(core):
        return pl.ds(pl.multiple_of(core * 2 * rows, 2 * rows), 2 * rows)

    at.meet()

    relay_dev = (y, z, 2 * y + c)
    over_dev = (y, z, 2 * (1 - y) + c)
    stays = both(c == y, r == c)

    def launch(g):
        i = GROUPS.index(g)
        goal = vmem[g].at[r, here, :]

        @pl.when(stays)
        def _():
            pltpu.make_async_copy(shard[g], goal, x_sem.at[i, r]).start()

        @pl.when(jnp.logical_not(stays))
        def _():
            push(shard[g], goal, x_sent.at[i], x_sem.at[i, r], relay_dev).start()

    def launch_over(g):
        i = GROUPS.index(g)
        return push(shard[g], vmem[g].at[r, here, :], y0_sent.at[i], yw_got.at[i, 0, r], over_dev)

    crs_dev = (y, z, 2 * y + 1)
    crs_stays = both(c == y, r == 1)

    def crs_goal(block, section):
        return crs_v.at[block, here, pl.ds(pl.multiple_of((1 - section) * side, side), side)]

    def launch_crs():
        @pl.when(crs_stays)
        def _():
            pltpu.make_async_copy(crs_in, crs_goal(r, c), c_sem.at[r, c]).start()

        @pl.when(jnp.logical_not(crs_stays))
        def _():
            push(crs_in, crs_goal(r, c), x_sent.at[1], c_sem.at[r, c], crs_dev).start()

    row_goal = s_v.at[strip(t, rows), :]
    cot_goal = cot.at[strip(t, rows), :]

    def row_stays(s):
        return both(both(c == y, r == c), y == s)

    def launch_rows(s):
        dev = (y, z, 2 * s + c)

        @pl.when(row_stays(s))
        def _():
            pltpu.make_async_copy(x_in.at[s], row_goal, row_got.at[r]).start()

        @pl.when(jnp.logical_not(row_stays(s)))
        def _():
            push(x_in.at[s], row_goal, row_sent.at[s], row_got.at[r], dev).start()

    def launch_cot():
        dev = (y, z, 2 * c + 1)

        @pl.when(crs_stays)
        def _():
            pltpu.make_async_copy(cot_in.at[c], cot_goal, cot_got.at[r]).start()

        @pl.when(jnp.logical_not(crs_stays))
        def _():
            push(cot_in.at[c], cot_goal, row_sent.at[2], cot_got.at[r], dev).start()

    gain_copy = push(gain_in, gain_in_v.at[c], gain_sem.at[0], gain_sem.at[1], at.twin)
    gain_copy.start()
    launch("att")
    launch_over("att").start()
    launch_rows(0)
    launch_rows(1)
    launch("up")
    launch_over("up").start()
    launch_crs()
    launch("dn")
    launch_cot()

    place = subs((slot, TILE))
    seen = jnp.where(y == 0, task_mask[0:1, :], task_mask[1:2, :]) == 1
    seen = jnp.broadcast_to(jnp.where(seen, 1.0, 0.0), (TILE, slot)).T > 0.5
    bias_self[...] = jnp.where(place < lengths[r, y], 0.0, NEG_FILL).astype(LOW)
    bias_cross[...] = jnp.where(both(place < lengths[0, y], seen), 0.0, NEG_FILL).astype(LOW)

    def piece(g, k, b):
        j = lax.rem(z - k + planes, planes)
        return vmem[g].at[b, pl.ds(pl.multiple_of(j * depth, depth), depth), :]

    def ring(g, k, b):
        i = GROUPS.index(g)
        return push(
            piece(g, k - 1, b), piece(g, k - 1, b), zw_sent.at[i, k - 1, b], zw_got.at[i, k - 1, b], at.above
        )

    def ring_in(g, k, b):
        i = GROUPS.index(g)
        return push(piece(g, k, b), piece(g, k, b), zw_sent.at[i, k - 1, b], zw_got.at[i, k - 1, b], at.above)

    def cross_over(g, k, b):
        i = GROUPS.index(g)
        return push(piece(g, k, b), piece(g, k, b), yw_sent.at[i, k, b], yw_got.at[i, k, b], at.across)

    def arrive(g, k, b):
        if k:
            ring_in(g, k, b).wait_recv()
        elif g == "crs":
            for section in range(2):
                goal = crs_goal(b, section)
                push(goal, goal, x_sent.at[1], c_sem.at[b, section], at.twin).wait_recv()
        else:
            i = GROUPS.index(g)
            goal = vmem[g].at[b, here, :]
            push(goal, goal, x_sent.at[i], x_sem.at[i, b], at.twin).wait_recv()

    def passing(g, k, up=True, over=True):
        skips = [b for b in range(2) if k == 1 and (g, b) in ASIDE]

        def half(b):
            if up:
                with jax.named_scope("await_" + g + str(k)):
                    arrive(g, k, b)
                if k + 1 < planes:
                    ring(g, k + 1, b).start()
            if over and not (k == 0 and g in DIRECT):
                if skips:
                    pl.when(b != skips[0])(lambda: cross_over(g, k, b).start())
                else:
                    cross_over(g, k, b).start()

        def run():
            each(2, half, "pass_" + g)

        return run

    def schedule(order):
        events = []
        for n, g in enumerate(order):
            for k in range(planes):
                if k == 0 and n == 0:
                    events.append(passing(g, 0))
                elif k:
                    events.append(passing(g, k))
                if n + 1 < len(order):
                    if k == planes - 2:
                        events[-1] = chained(events[-1], passing(order[n + 1], 0, True, False))
                    if k == planes - 1:
                        events[-1] = chained(events[-1], passing(order[n + 1], 0, False, True))
        return events

    def chained(one, two):
        def run():
            one()
            two()

        return run

    enc_events = schedule(("att", "up", "dn"))
    dec_events = schedule(("att", "crs", "up", "dn"))

    def pump_enc(count):
        for _ in range(min(count, len(enc_events))):
            pl.when(both(relay, at.encodes))(enc_events.pop(0))

    def pump_dec(count):
        for _ in range(min(count, len(dec_events))):
            pl.when(both(relay, at.decodes))(dec_events.pop(0))

    def pump(count):
        pump_enc(count)
        pump_dec(count)

    def side_hop(g, b):
        i = GROUPS.index(g)
        return push(piece(g, 0, b), piece(g, 0, b), side_sent.at[i, b], side_got.at[i, b], at.above)

    def side_in(g, b):
        i = GROUPS.index(g)
        return push(piece(g, 1, b), piece(g, 1, b), side_sent.at[i, b], side_got.at[i, b], at.above)

    def pass_aside(g):
        @pl.when(other)
        def _():
            for b in range(2):
                cross_over(g, 0, b).wait_recv()
                if (g, b) in ASIDE:
                    side_hop(g, b).start()

    def settle(g):
        listens = both(other, at.decodes) if g == "crs" else other

        @pl.when(listens)
        @jax.named_scope("settle_" + g)
        def _():
            for k in range(planes):
                for b in range(2):
                    if k == 1 and (g, b) in ASIDE:
                        side_in(g, b).wait_recv()
                    elif k or g in ("att", "crs"):
                        cross_over(g, k, b).wait_recv()

    def exchange(e, i):
        q = strip(i, BLOCK)
        k = e % 2
        return push(send_v.at[k, q, :], recv_v.at[k, q, :], ex_sent.at[e, i], ex_got.at[e, i], at.twin)

    def joined(e, i):
        q = strip(i, BLOCK)
        exchange(e, i).wait_recv()
        return send_v[e % 2, q, :].astype(WIDE) + recv_v[e % 2, q, :].astype(WIDE)

    def sent(e):
        each(tiles, lambda i: exchange(e, i).wait_send())

    pump(3)
    for k in range(2):
        goal = s_v.at[strip(2 * c + k, rows), :]
        push(goal, goal, row_sent.at[0], row_got.at[k], at.twin).wait_recv()
    half, far_half = half_of(c), half_of(1 - c)
    rows_on = push(s_v.at[half, :], s_v.at[half, :], fwd_sem.at[0], fwd_sem.at[1], at.twin)
    rows_on.start()
    push(gain_in, gain_in_v.at[1 - c], gain_sem.at[0], gain_sem.at[1], at.twin).wait_recv()
    gain_here = pltpu.make_async_copy(gain_in, gain_in_v.at[c], gain_sem.at[2])
    gain_here.start()
    gain_here.wait()
    gains = gain_in_v[r].astype(WIDE)
    g0, g1, g2 = gains[0:1, :], gains[1:2, :], gains[2:3, :]
    gain_v[...] = jnp.zeros_like(gain_v)
    push(s_v.at[far_half, :], s_v.at[far_half, :], fwd_sem.at[0], fwd_sem.at[1], at.twin).wait_recv()
    x_put = copying("x", s_v, x_k)
    x_put.start()

    def enter(i):
        q = strip(i, BLOCK)
        c_v[q, :] = (center(s_v[q, :].astype(WIDE))[0] * g0).astype(LOW)

    each(tiles, enter)
    first_put = copying("first", c_v, first_k)
    first_put.start()
    pump(1)
    settle("att")

    def project(source, weights, part):
        def project_rows(n):
            b, q = lax.rem(n, 2), strip(lax.div(n, 2), BLOCK)
            if part != "kv":
                a_v[b, q, 0:256] = mm(source[q, :], weights[b, :, 0:256]).astype(LOW)
            if part != "q":
                a_v[b, q, 256:640] = mm(source[q, :], weights[b, :, 384:768]).astype(LOW)

        each(2 * tiles, project_rows)

    packed_v = a_v.at[:, :, 0:640]
    project(c_v, att_v, "all")
    pass_aside("up")
    p_put = copying("p", packed_v, p_k)
    p_put.start()
    o_v[...] = jnp.zeros_like(o_v)
    lse_v[...] = jnp.zeros_like(lse_v)
    pump(1)

    def attend_heads(bias, causal, hooks):
        def head_forward(n):
            b = lax.div(n, 3)
            attend_block(lax.rem(n, 3), a_v.at[b], o_v.at[b], lse_v, n, bias, kx, qx, kt_v, causal)
            for when, event in hooks:
                pl.when(both(n == when, relay))(event)

        each(6, head_forward)

    enc_hooks = [(2, enc_events.pop(0)), (5, enc_events.pop(0))]
    dec_hooks = [(2, dec_events.pop(0)), (4, dec_events.pop(0))]
    pl.when(at.encodes)(lambda: attend_heads(bias_self, False, enc_hooks))
    pl.when(at.decodes)(lambda: attend_heads(bias_self, True, dec_hooks))
    o_put, lse_put = copying("o", o_v, o_k), copying("lse", lse_v, lse_k)
    o_put.start()
    lse_put.start()

    def out_project(e, weights):
        def out_rows(i):
            q = strip(i, BLOCK)
            part = mm_nt(o_v[0, q, :], weights[0, :, 128:384]) + mm_nt(o_v[1, q, :], weights[1, :, 128:384])
            send_v[e % 2, q, :] = part.astype(LOW)
            exchange(e, i).start()

        each(tiles, out_rows)

    out_project(0, att_v)
    pump(1)
    x_put.wait()
    pass_aside("dn")
    rows_on.wait_send()

    def middle(i):
        q = strip(i, BLOCK)
        value = s_v[q, :].astype(WIDE) + joined(0, i)
        mid_v[q, :] = value
        s_v[q, :] = (center(value)[0] * g1).astype(LOW)

    each(tiles, middle)
    first_put.wait()
    p_put.wait()
    o_put.wait()
    lse_put.wait()

    def mem_send(i):
        q = pl.ds(pl.multiple_of((2 * c + i) * BLOCK, BLOCK), BLOCK)
        return push(g_v.at[q, :], g_v.at[q, :], mem_sent.at[i], mem_got.at[i], at.beside)

    def mem_forward(i, core):
        q = pl.ds(pl.multiple_of((2 * core + i) * BLOCK, BLOCK), BLOCK)
        return push(g_v.at[q, :], g_v.at[q, :], mf_sent.at[i], mf_got.at[i], at.twin)

    def row_home(k, source, goal, sent_by, got):
        dev = (r, z, 2 * c + k)
        keeps = both(both(c == r, y == c), r == k)
        return keeps, source, goal.at[y], sent_by.at[k], got.at[y], dev

    def go_home(*spec):
        keeps, source, goal, sent_by, got, dev = row_home(*spec)

        @pl.when(keeps)
        def _():
            pltpu.make_async_copy(source, goal, got).start()

        @pl.when(jnp.logical_not(keeps))
        def _():
            push(source, goal, sent_by, got, dev).start()

    def went_home(*spec):
        keeps, source, goal, sent_by, got, dev = row_home(*spec)

        @pl.when(jnp.logical_not(keeps))
        def _():
            push(source, goal, sent_by, got, dev).wait_send()

    def memory_home(k):
        return k, memory_k.at[strip(2 * c + k, rows), :], block_out, blk_sent, blk_got

    settle_up = lambda: settle("up")
    pl.when(at.encodes)(settle_up)

    @pl.when(at.encodes)
    def _():
        def up_rows(n):
            b, q = lax.rem(n, 2), strip(lax.div(n, 2), BLOCK)
            value, grade = gelu_parts(mm(s_v[q, :], up_v[b]))
            a_v[b, q, :] = value.astype(LOW)
            b_v[b, q, :] = grade.astype(LOW)

        each(2 * tiles, up_rows)

    pump_enc(9)

    @pl.when(at.encodes)
    def _():
        settle("dn")

        def down_rows(i):
            q = strip(i, BLOCK)
            part = mm_nt(a_v[0, q, :], dn_v[0]) + mm_nt(a_v[1, q, :], dn_v[1])
            send_v[1, q, :] = part.astype(LOW)
            exchange(1, i).start()

        each(tiles, down_rows)

        def finish(n):
            i = lax.rem(n + 2 * c, 4)
            q = strip(i, BLOCK)
            value = mid_v[q, :] + joined(1, i)
            late_v[q, :] = value
            g_v[q, :] = (center(value)[0] * g2).astype(LOW)

            @pl.when(n < 2)
            def _():
                mem_send(n).start()

        each(tiles, finish)
        keep = copying("memory", g_v, memory_k)
        keep.start()
        keep.wait()
        for k in range(2):
            go_home(*memory_home(k))
        sent(0)

    def norm_grad(values, gain, grad, gain_row, counted):
        normal, scale = center(values)
        scaled = grad * gain
        one = jnp.mean(scaled, axis=-1, keepdims=True)
        two = jnp.mean(scaled * normal, axis=-1, keepdims=True)
        total = jnp.sum(grad * normal, axis=0, keepdims=True)
        gain_v[gain_row : gain_row + 1, :] += jnp.where(counted, total, 0.0)
        return (scaled - one - normal * two) * scale

    def ours(i):
        return lax.div(i, 2) == c

    @pl.when(at.decodes)
    def _():
        second_put = copying("second", s_v, second_k)
        second_put.start()
        for k in range(2):
            goal = cot.at[strip(2 * c + k, rows), :]
            push(goal, goal, row_sent.at[2], cot_got.at[k], at.twin).wait_recv()
        cot_on = push(cot.at[half, :], cot.at[half, :], fwd_sem.at[2], fwd_sem.at[3], at.twin)
        cot_on.start()
        for _ in range(len(dec_events) - 3):
            pl.when(relay)(dec_events.pop(0))
        settle("crs")
        project(s_v, crs_v, "q")
        pl.when(relay)(dec_events.pop(0))
        pl.when(relay)(dec_events.pop(0))
        push(cot.at[far_half, :], cot.at[far_half, :], fwd_sem.at[2], fwd_sem.at[3], at.twin).wait_recv()
        cot_in_v = copying("cot", cot, c_v)
        cot_in_v.start()
        o_v[...] = jnp.zeros_like(o_v)
        lse_v[...] = jnp.zeros_like(lse_v)
        for i in range(2):
            mem_send(i).wait_recv()
            mem_forward(i, c).start()
        for i in range(2):
            mem_forward(i, 1 - c).wait_recv()
        project(g_v, crs_v, "kv")
        puts = [copying("pc", packed_v, pc_k), copying("memory", g_v, memory_k)]
        for copy in puts:
            copy.start()
        attend_heads(bias_cross, False, [(0, dec_events.pop(0))])
        puts += [copying("oc", o_v, oc_k), copying("lsec", lse_v, lsec_k)]
        for copy in puts[2:]:
            copy.start()
        out_project(1, crs_v)
        second_put.wait()

        def finish(i):
            q = strip(i, BLOCK)
            value = mid_v[q, :] + joined(1, i)
            late_v[q, :] = value
            s_v[q, :] = (center(value)[0] * g2).astype(LOW)

        each(tiles, finish)
        late_put = copying("late", late_v, late_k)
        late_put.start()
        settle("up")
        settle("dn")
        cot_in_v.wait()
        sent(0)
        for copy in puts:
            copy.wait()

        def feed_rows(i):
            q = strip(i, BLOCK)

            def feed_half(b):
                value, grade = gelu_parts(mm(s_v[q, :], up_v[b]))
                a_v[b, q, :] = value.astype(LOW)
                b_v[b, q, :] = (mm(c_v[q, :], dn_v[b]) * grade).astype(LOW)

            each(2, feed_half)
            part = mm_nt(b_v[0, q, :], up_v[0]) + mm_nt(b_v[1, q, :], up_v[1])
            send_v[0, q, :] = part.astype(LOW)
            exchange(2, i).start()

        each(tiles, feed_rows)
        copying("act", a_v, act_k).start()
        late_put.wait()
        cot_on.wait_send()
        each(2, lambda i: mem_forward(i, c).wait_send())

    def block_of(k):
        return lax.rem(z - 1 - k + 2 * planes, planes)

    def y_hop(g, k, b):
        i = SUMS.index(g)
        return push(dw[g].at[k, b], yb[g].at[k, b], y_sent.at[i, k, b], y_got.at[i, k, b], at.across)

    def z_hop(g, k, b):
        i = SUMS.index(g)
        return push(dw[g].at[k, b], zb[g].at[k, b], z_sent.at[i, k, b], z_got.at[i, k, b], at.above)

    def leave(g, k):
        @pl.when(other)
        def _():
            for b in range(2):
                y_hop(g, k, b).start()

    def emit(g, compute):
        columns = dw[g].shape[3]

        def put(k, s):
            return pltpu.make_async_copy(dw_st.at[s, :, :, 0:columns], dw[g].at[k], dw_sem.at[s])

        def run(k):
            s = lax.rem(k, 2)
            j = block_of(k)
            compute(s, pl.ds(pl.multiple_of(j * depth, depth), depth))
            put(k, s).start()

            @pl.when(k >= 1)
            def _():
                put(k - 1, 1 - s).wait()
                leave(g, k - 1)

        each(planes, run, "emit_" + g)
        put(planes - 1, (planes - 1) % 2).wait()
        leave(g, planes - 1)

    def home_copy(g, b, section):
        i = SUMS.index(g)
        columns = dw[g].shape[3]
        source = dw[g].at[planes - 1, b]
        if g == "crs":
            source = source.at[:, pl.ds((1 - section) * (columns // 2), columns // 2)]
        device = (section, z, 2 * y + b)
        keeps = both(c == section, r == b)
        return keeps, source, push(source, home[g], home_sent.at[i, b, section if g == "crs" else 0], home_got.at[i], device)

    def sections(g):
        return (0, 1) if g == "crs" else (r,)

    def sum_at(g, n):
        i = SUMS.index(g)
        columns = dw[g].shape[3]
        k, b = lax.div(n, 2), lax.rem(n, 2)

        def fetch(m, source):
            return pltpu.make_async_copy(source, sum_st.at[m, :, 0:columns], sum_sem.at[m])

        @pl.when(relay)
        @jax.named_scope("sum_" + g)
        def _():
            before = lax.max(k - 1, 0)
            y_hop(g, k, b).wait_recv()
            fetch(0, dw[g].at[k, b]).start()
            fetch(1, yb[g].at[k, b]).start()

            @pl.when(k > 0)
            def _():
                z_hop(g, before, b).wait_recv()
                fetch(2, zb[g].at[before, b]).start()
                fetch(2, zb[g].at[before, b]).wait()

            fetch(0, dw[g].at[k, b]).wait()
            fetch(1, yb[g].at[k, b]).wait()
            share = depth // 4

            def add_rows(m):
                q = strip(m, share)
                total = sum_st[0, q, 0:columns].astype(WIDE) + sum_st[1, q, 0:columns].astype(WIDE)
                total = total + jnp.where(k > 0, sum_st[2, q, 0:columns].astype(WIDE), 0.0)
                sum_st[0, q, 0:columns] = total.astype(LOW)

            each(4, add_rows)
            back = pltpu.make_async_copy(sum_st.at[0, :, 0:columns], dw[g].at[k, b], sum_sem.at[0])
            back.start()
            back.wait()

            @pl.when(k + 1 < planes)
            def _():
                z_hop(g, k, b).start()

            @pl.when(k + 1 == planes)
            def _():
                for section in sections(g):
                    keeps, source, copy = home_copy(g, b, section)

                    @pl.when(keeps)
                    def _():
                        pltpu.make_async_copy(source, home[g], home_got.at[i]).start()

                    @pl.when(jnp.logical_not(keeps))
                    def _():
                        copy.start()

    def sums(g, first_step, count):
        each(count, lambda n: sum_at(g, first_step + n), "sums_" + g)

    def turn(source, goal):
        def run(i):
            q = strip(i, BLOCK)
            goal[:, q] = source[q, :].astype(WIDE).T.astype(LOW)

        each(tiles, run, "turn")

    def dm_hop(n, source):
        q = pl.ds(pl.multiple_of((2 * c + n) * BLOCK, BLOCK), BLOCK)
        return push(source.at[q, :], c_v.at[q, :], dm_sent.at[n], dm_got.at[n], at.beside)

    def df_hop(n, core):
        q = pl.ds(pl.multiple_of((2 * core + n) * BLOCK, BLOCK), BLOCK)
        return push(c_v.at[q, :], c_v.at[q, :], df_sent.at[n], df_got.at[n], at.twin)

    @pl.when(at.encodes)
    def _():
        def back_rows(m):
            n = lax.div(m, 2)
            own = lax.rem(m, 2) == 0
            i = jnp.where(own, 2 * c + n, 2 * (1 - c) + n)
            q = strip(i, BLOCK)

            @pl.when(own)
            def _():
                dm_hop(n, c_v).wait_recv()
                df_hop(n, c).start()

            @pl.when(jnp.logical_not(own))
            def _():
                df_hop(n, 1 - c).wait_recv()

            grad = norm_grad(late_v[q, :], g2, c_v[q, :].astype(WIDE), 2, ours(i))
            late_v[q, :] = grad
            low = grad.astype(LOW)
            part = None
            for b in range(2):
                d_pre = (mm(low, dn_v[b]) * b_v[b, q, :].astype(WIDE)).astype(LOW)
                b_v[b, q, :] = d_pre
                term = mm_nt(d_pre, up_v[b])
                part = term if part is None else part + term
            send_v[0, q, :] = part.astype(LOW)

            @pl.when(own)
            def _():
                df_hop(n, c).wait_send()

            c_v[q, :] = low
            exchange(2, i).start()

        each(tiles, back_rows)

    turn(s_v, ta)
    turn(c_v, tb)

    def ffn_block(s, j):
        def ffn_half(b):
            dw_st[s, b, :, 0:768] = mm(ta[j, :], b_v[b]).astype(LOW)
            dw_st[s, b, :, 768:1536] = mm(tb[j, :], a_v[b]).astype(LOW)

        each(2, ffn_half)

    emit("ffn", ffn_block)

    @pl.when(at.decodes)
    def _():
        copying("act", a_v, act_k).wait()
        packed = copying("pc", pc_k, packed_v)
        small = [copying("oc", oc_k, o_v), copying("lsec", lsec_k, lse_v), copying("second", second_k, s_v)]
        packed.start()
        for copy in small:
            copy.start()

        def late_rows(i):
            q = strip(i, BLOCK)
            grad = c_v[q, :].astype(WIDE) + norm_grad(late_v[q, :], g2, joined(2, i), 2, ours(i))
            late_v[q, :] = grad
            g_v[q, :] = grad.astype(LOW)

        each(tiles, late_rows)

        def cross_out(i):
            q = strip(i, BLOCK)
            for b in range(2):
                do_v[b, q, :] = mm(g_v[q, :], crs_v[b, :, 128:384]).astype(LOW)

        each(tiles, cross_out)
        for copy in small:
            copy.wait()
        packed.wait()
        b_v[...] = jnp.zeros_like(b_v)

        def cross_head(n):
            b = lax.div(n, 3)
            attend_back_block(
                lax.rem(n, 3), a_v.at[b], o_v.at[b], do_v.at[b], b_v.at[b], lse_v, n, bias_cross,
                kx, qx, vx, gx, kt_v, dk_v, dv_v, False,
            )

        each(6, cross_head)
        sent(1)

        def to_memory(q):
            return mm_nt(b_v[0, q, 256:640], crs_v[0, :, 384:768]) + mm_nt(b_v[1, q, 256:640], crs_v[1, :, 384:768])

        def far(n):
            i = 2 * (1 - c) + n
            q = strip(i, BLOCK)
            send_v[1, q, :] = to_memory(q).astype(LOW)
            exchange(3, i).start()

        each(2, far)

        def near(n):
            i = 2 * c + n
            q = strip(i, BLOCK)
            part = to_memory(q)
            exchange(3, i).wait_recv()
            send_v[1, q, :] = (part + recv_v[1, q, :].astype(WIDE)).astype(LOW)
            dm_hop(n, send_v.at[1]).start()

        each(2, near)

        def to_query(i):
            q = strip(i, BLOCK)
            part = mm_nt(b_v[0, q, 0:256], crs_v[0, :, 0:256]) + mm_nt(b_v[1, q, 0:256], crs_v[1, :, 0:256])
            send_v[0, q, :] = part.astype(LOW)
            exchange(4, i).start()

        sent(2)
        each(tiles, to_query)
        sums("ffn", 0, 2)
        turn(s_v, ta)
        stage_in = copying("memory", memory_k, s_v)
        stage_in.start()
        turn(g_v, tc)
        stage_in.wait()
        turn(s_v, tb)
        copying("first", first_k, s_v).start()

        def crs_block(s, j):
            def att_half(b):
                left = mm(ta[j, :], b_v[b, :, 0:256])
                out = mm(tc[j, :], o_v[b])
                dw_st[s, b, :, 0:128] = left[:, 0:128].astype(LOW)
                dw_st[s, b, :, 128:256] = (left[:, 128:256] + out[:, 0:128]).astype(LOW)
                dw_st[s, b, :, 256:384] = out[:, 128:256].astype(LOW)
                dw_st[s, b, :, 384:768] = mm(tb[j, :], b_v[b, :, 256:640]).astype(LOW)

            each(2, att_half)

        emit("crs", crs_block)
        sums("ffn", 2, 2)

        def below(i):
            q = strip(i, BLOCK)
            grad = late_v[q, :] + norm_grad(mid_v[q, :], g1, joined(4, i), 1, ours(i))
            late_v[q, :] = grad
            g_v[q, :] = grad.astype(LOW)

        each(tiles, below)
        copying("first", first_k, s_v).wait()

        def gone(n):
            exchange(3, 2 * (1 - c) + n).wait_send()
            dm_hop(n, send_v.at[1]).wait_send()

        each(2, gone)

    @pl.when(at.encodes)
    def _():
        copying("first", first_k, s_v).start()
        each(2, lambda i: mem_send(i).wait_send())

        def below(i):
            q = strip(i, BLOCK)
            grad = late_v[q, :] + norm_grad(mid_v[q, :], g1, joined(2, i), 1, ours(i))
            late_v[q, :] = grad
            g_v[q, :] = grad.astype(LOW)

        each(tiles, below)
        copying("first", first_k, s_v).wait()
        sent(1)

    packed = copying("p", p_k, packed_v)
    small = [copying("o", o_k, o_v), copying("lse", lse_k, lse_v)]
    packed.start()
    for copy in small:
        copy.start()

    def self_out(i):
        q = strip(i, BLOCK)
        for b in range(2):
            do_v[b, q, :] = mm(g_v[q, :], att_v[b, :, 128:384]).astype(LOW)

    each(tiles, self_out)
    b_v[...] = jnp.zeros_like(b_v)
    for copy in small:
        copy.wait()
    packed.wait()

    def self_heads(causal, hook):
        def self_head(n):
            b = lax.div(n, 3)
            attend_back_block(
                lax.rem(n, 3), a_v.at[b], o_v.at[b], do_v.at[b], b_v.at[b], lse_v, n, bias_self,
                kx, qx, vx, gx, kt_v, dk_v, dv_v, causal,
            )
            hook(n)

        each(6, self_head)

    def enc_hook(n):
        @pl.when(jnp.logical_and(n != 0, n != 3))
        def _():
            sum_at("ffn", n - 1 - lax.div(n, 4))

    def dec_hook(n):
        @pl.when(n < 4)
        def _():
            sum_at("ffn", 4 + n)

        @pl.when(n >= 4)
        def _():
            sum_at("crs", n - 4)

    pl.when(at.encodes)(lambda: self_heads(False, enc_hook))
    pl.when(at.decodes)(lambda: self_heads(True, dec_hook))

    def to_rows(q):
        part = None
        for b in range(2):
            term = mm_nt(b_v[b, q, 0:256], att_v[b, :, 0:256]) + mm_nt(b_v[b, q, 256:640], att_v[b, :, 384:768])
            part = term if part is None else part + term
        return part

    def far_rows(n):
        i = 2 * (1 - c) + n
        q = strip(i, BLOCK)
        send_v[1, q, :] = to_rows(q).astype(LOW)
        exchange(5, i).start()

    each(2, far_rows)
    turn(s_v, ta)
    x_in_v = copying("x", x_k, s_v)
    x_in_v.start()
    turn(g_v, tc)

    def att_block(s, j):
        def att_half(b):
            left = mm(ta[j, :], b_v[b, :, 0:256])
            out = mm(tc[j, :], o_v[b])
            dw_st[s, b, :, 0:128] = left[:, 0:128].astype(LOW)
            dw_st[s, b, :, 128:256] = (left[:, 128:256] + out[:, 0:128]).astype(LOW)
            dw_st[s, b, :, 256:384] = out[:, 128:256].astype(LOW)
            dw_st[s, b, :, 384:768] = mm(ta[j, :], b_v[b, :, 256:640]).astype(LOW)

        each(2, att_half)

    emit("att", att_block)
    pl.when(at.encodes)(lambda: sums("ffn", 4, 2))
    pl.when(at.decodes)(lambda: sums("crs", 2, 2))
    x_in_v.wait()

    def near_rows(n):
        i = 2 * c + n
        q = strip(i, BLOCK)
        part = to_rows(q)
        exchange(5, i).wait_recv()
        grad = part + recv_v[1, q, :].astype(WIDE)
        value = late_v[q, :] + norm_grad(s_v[q, :].astype(WIDE), g0, grad, 0, True)
        out_st[strip(n, BLOCK), :] = value.astype(LOW)

    each(2, near_rows)
    out_put = copying("out", out_st, grad_k)
    out_put.start()
    out_put.wait()

    def grad_home(k):
        return k, grad_k.at[strip(k, rows), :], grad_low, gr_sent, gr_got

    for k in range(2):
        go_home(*grad_home(k))

    def gain_hop(n, source, device):
        return push(source, gain_buf.at[n], gr_hop_sent.at[n], gr_hop_got.at[n], device)

    gain_buf[0] = gain_v[...]
    twin_hop = gain_hop(1, gain_buf.at[0], at.twin)
    twin_hop.start()
    twin_hop.wait()
    peer_hop = gain_hop(3, gain_buf.at[2], (1 - c, z, lax.rem(t + 2, 4)))
    last = 4 + planes

    @pl.when(relay)
    def _():
        gain_buf[2] = gain_buf[0] + gain_buf[1]
        peer_hop.start()

    def ring_hop(n):
        return gain_hop(5 + n, gain_buf.at[4 + n], at.above)

    def gain_step(n):
        @pl.when(relay)
        @jax.named_scope("gains")
        def _():
            if n == 0:
                peer_hop.wait()
                gain_buf[4] = gain_buf[2] + gain_buf[3]
            else:
                ring_hop(n - 1).wait()
            if n < planes - 1:
                ring_hop(n).start()
            else:
                total = None
                for j in range(planes):
                    held = gain_buf[jnp.where(z == j, 4, 5 + lax.rem(z - 1 - j + planes, planes))]
                    total = held if total is None else total + held
                gain_buf[last] = total
                for b in range(2):
                    keeps = both(c == r, r == b)

                    @pl.when(keeps)
                    def _():
                        pltpu.make_async_copy(gain_buf.at[last], gain_buf.at[last + 1], gr_hop_got.at[last + 1]).start()

                    @pl.when(jnp.logical_not(keeps))
                    def _():
                        final_hop(b).start()

    def final_hop(b):
        return push(
            gain_buf.at[last], gain_buf.at[last + 1], gr_hop_sent.at[last + b], gr_hop_got.at[last + 1],
            (r, z, 2 * y + b),
        )

    def y3_home(k):
        return k, y3_k.at[strip(k, rows), :], block_out, blk_sent, blk_got

    @pl.when(at.decodes)
    def _():
        copies = [copying("act", act_k, a_v), copying("late", late_k, mid_v)]
        for copy in copies:
            copy.start()
        sent(4)
        for copy in copies:
            copy.wait()

        def to_out(q):
            return mm_nt(a_v[0, q, :], dn_v[0]) + mm_nt(a_v[1, q, :], dn_v[1])

        def far_out(n):
            i = 2 * (1 - c) + n
            q = strip(i, BLOCK)
            send_v[0, q, :] = to_out(q).astype(LOW)
            exchange(6, i).start()

        each(2, far_out)

        def near_out(n):
            i = 2 * c + n
            q = strip(i, BLOCK)
            part = to_out(q)
            exchange(6, i).wait_recv()
            out_st[strip(n, BLOCK), :] = (mid_v[q, :] + part + recv_v[0, q, :].astype(WIDE)).astype(LOW)

        each(2, near_out)
        y3_put = copying("out", out_st, y3_k)
        y3_put.start()
        y3_put.wait()
        for k in range(2):
            go_home(*y3_home(k))

    pl.when(at.encodes)(lambda: sums("ffn", 6, 2))
    pl.when(at.decodes)(lambda: sums("crs", 4, 4))

    def last_sums(n):
        sum_at("att", n)
        for m in range(planes):
            pl.when(n == m)(functools.partial(gain_step, m))

    each(2 * planes, last_sums)

    with jax.named_scope("await_gains"):
        final = gain_buf.at[last + 1]
        push(gain_buf.at[last], final, gr_hop_sent.at[last], gr_hop_got.at[last + 1], at.twin).wait_recv()
    gains_home = copying("gains", final, gain_out)
    gains_home.start()
    with jax.named_scope("await_rows"):
        for n in range(2):
            for goal, got in ((block_out, blk_got), (grad_low, gr_got)):
                push(goal.at[n], goal.at[n], blk_sent.at[0], got.at[n], at.twin).wait_recv()
    for i, g in enumerate(SUMS):
        with jax.named_scope("await_home_" + g):
            push(home[g], home[g], home_sent.at[i, 0, 0], home_got.at[i], at.twin).wait_recv()
    gains_home.wait()
    for k in range(2):
        went_home(*grad_home(k))

    @pl.when(at.encodes)
    def _():
        for k in range(2):
            went_home(*memory_home(k))
        sent(2)

    @pl.when(at.decodes)
    def _():
        for k in range(2):
            went_home(*y3_home(k))
        each(2, lambda n: exchange(6, 2 * (1 - c) + n).wait_send())

    each(2, lambda n: exchange(5, 2 * (1 - c) + n).wait_send())

    @pl.when(relay)
    def _():
        for b in range(2):
            pl.when(jnp.logical_not(both(c == r, r == b)))(lambda: final_hop(b).wait_send())

    for g in SUMS:
        there = at.decodes if g == "crs" else jnp.logical_or(at.decodes, at.encodes)

        @pl.when(both(other, there))
        def _():
            for k in range(planes):
                for b in range(2):
                    y_hop(g, k, b).wait_send()

        @pl.when(both(relay, there))
        def _():
            for b in range(2):
                for k in range(planes - 1):
                    z_hop(g, k, b).wait_send()
                for section in sections(g):
                    keeps, source, copy = home_copy(g, b, section)

                    @pl.when(jnp.logical_not(keeps))
                    def _():
                        copy.wait_send()

    gain_copy.wait_send()
    for g in DIRECT:
        launch_over(g).wait_send()

    @pl.when(jnp.logical_not(stays))
    def _():
        for g in ("att", "up", "dn"):
            push(shard[g], vmem[g].at[r, here, :], x_sent.at[GROUPS.index(g)], x_sem.at[0, 0], relay_dev).wait_send()

    @pl.when(jnp.logical_not(crs_stays))
    def _():
        push(crs_in, crs_goal(r, c), x_sent.at[1], c_sem.at[0, 0], crs_dev).wait_send()
        push(cot_in.at[c], cot_goal, row_sent.at[2], cot_got.at[r], at.twin).wait_send()

    for s in range(2):

        @pl.when(jnp.logical_not(row_stays(s)))
        def _():
            push(x_in.at[s], row_goal, row_sent.at[s], row_got.at[r], at.twin).wait_send()

    for g in GROUPS:
        member = both(relay, at.decodes) if g == "crs" else relay

        @pl.when(member)
        def _():
            for k in range(planes):
                for b in range(2):
                    if k:
                        ring(g, k, b).wait_send()
                    if (k or g not in DIRECT) and (k != 1 or (g, b) not in ASIDE):
                        cross_over(g, k, b).wait_send()

    @pl.when(other)
    def _():
        for g, b in ASIDE:
            side_hop(g, b).wait_send()


def block_call(planes, slot, width, hidden, depth, args):
    shape = jax.ShapeDtypeStruct
    rows = slot // 4
    square = (slot, width)
    wides = {"ffn": 2 * hidden, "crs": width, "att": width}
    packed, outs, logs, acts = (2, slot, 640), (2, slot, 256), (8, slot), (2, slot, hidden)
    out_shape = (
        [shape((2, rows, width), LOW)] * 2
        + [shape((depth, 2 * hidden), LOW), shape((depth, width // 2), LOW), shape((depth, width), LOW)]
        + [shape((8, width), WIDE)]
        + [shape(square, LOW)] * 4
        + [shape(square, WIDE), shape(square, LOW)]
        + [shape(packed, LOW), shape(outs, LOW), shape(logs, WIDE)] * 2
        + [shape(acts, LOW)]
        + [shape((2 * rows, width), LOW)] * 2
        + [shape((planes, 2, depth, wides[g]), LOW) for g in SUMS] * 3
    )
    dma = pltpu.SemaphoreType.DMA
    v = pltpu.VMEM
    groups = len(GROUPS)
    scratch = (
        [v((2, width, width), LOW)] * 2
        + [v((2, width, hidden), LOW)] * 2
        + [v(acts, LOW)] * 2
        + [v(outs, LOW)] * 2
        + [v(square, WIDE)] * 2
        + [v(square, LOW)] * 3
        + [v((width, slot), LOW)] * 3
        + [v((2,) + square, LOW)] * 2
        + [v((slot, TILE), LOW)] * 4
        + [v((slot, TILE), WIDE)] * 2
        + [v((TILE, slot), LOW), v(logs, WIDE), v((8, width), WIDE), v((2, 3, width), LOW)]
        + [v((planes + 6, 8, width), WIDE)]
        + [v((2 * rows, width), LOW), v((2, 2, depth, 2 * hidden), LOW), v((3, depth, 2 * hidden), LOW)]
        + [v((slot, TILE), LOW)] * 2
        + [dma((groups, 2)), dma((groups,)), dma((groups,)), dma((2, 2))]
        + [dma((groups, planes, 2))] * 4
        + [dma((groups, 2))] * 2
        + [dma((2,)), dma((3,)), dma((4,)), dma((2,)), dma((3,)), dma((40,)), dma((7, 4)), dma((7, 4))]
        + [dma((2,))] * 8
        + [dma((3, planes, 2))] * 4
        + [dma((3,)), dma((3, 2, 2))]
        + [dma((2,))] * 4
        + [dma((planes + 6,))] * 2
        + [dma((3,)), dma((2,))]
    )
    any_spec = pl.BlockSpec(memory_space=pl.ANY)
    vmem_spec = pl.BlockSpec(memory_space=pltpu.VMEM)
    return pl.pallas_call(
        functools.partial(block_kernel, planes),
        out_shape=out_shape,
        in_specs=[any_spec] * 6 + [vmem_spec, pl.BlockSpec(memory_space=pltpu.SMEM), vmem_spec],
        out_specs=[any_spec] * len(out_shape),
        scratch_shapes=scratch,
        compiler_params=pltpu.CompilerParams(collective_id=0, has_side_effects=True, vmem_limit_bytes=VMEM_BYTES),
    )(*args)


def widen_kernel(
    block_in, grad_in, ffn_in, crs_in, att_in, gain_in,
    block_out, grad_out, up_out, dn_out, qkv_out, out_out, crs_out, gain_out, last_out,
):
    c = lax.axis_index("section")
    hidden = up_out.shape[1]
    share, part = block_in.shape[1] // 4, ffn_in.shape[0] // 4

    def strips(i):
        q = strip(i, share)
        for n in range(2):
            block_out[n, q, :] = block_in[n, q, :]
            grad_out[n, q, :] = grad_in[n, q, :].astype(WIDE)
        q = strip(i, part)
        up_out[q, :] = ffn_in[q, 0:hidden].astype(WIDE)
        dn_out[q, :] = ffn_in[q, hidden : 2 * hidden].astype(WIDE)

    each(4, strips)
    tiles = [crs_in[:, TILE * n : TILE * (n + 1)].astype(WIDE) for n in range(3)]
    mixed = jnp.where(c == 1, tiles[1], tiles[2])
    crs_out[0, :, 0:TILE] = tiles[0]
    crs_out[0, :, TILE : TILE + HEAD] = mixed[:, 0:HEAD]
    crs_out[1, :, 0:TILE] = jnp.where(c == 1, tiles[2], tiles[1])
    crs_out[1, :, TILE : TILE + HEAD] = pltpu.roll(mixed, HEAD, 1)[:, 0:HEAD]
    q_tile, q_o, o_tile, k_tile, v_tile, k_v = (att_in[:, TILE * n : TILE * (n + 1)].astype(WIDE) for n in range(6))
    for n, (whole, rest) in enumerate(((q_tile, q_o), (k_tile, k_v), (v_tile, pltpu.roll(k_v, HEAD, 1)))):
        qkv_out[n, :, 0:TILE] = whole
        qkv_out[n, :, TILE : TILE + HEAD] = rest[:, 0:HEAD]
    out_out[0:TILE, :] = o_tile.T
    out_out[TILE : TILE + HEAD, :] = pltpu.roll(q_o, HEAD, 1).T[0:HEAD, :]
    gain_out[...] = gain_in[0:2, :]
    last_out[...] = gain_in[2:3, :]


def widen_call(kept):
    shape = jax.ShapeDtypeStruct
    rows, width = kept[0].shape[1:]
    depth, hidden = kept[2].shape[0], kept[2].shape[1] // 2
    wide = width // 4
    return pl.pallas_call(
        widen_kernel,
        out_shape=[
            shape((2, rows, width), LOW), shape((2, rows, width), WIDE), shape((depth, hidden), WIDE),
            shape((depth, hidden), WIDE), shape((3, depth, wide), WIDE), shape((wide, depth), WIDE),
            shape((2, depth, wide), WIDE), shape((2, width), WIDE), shape((1, width), WIDE),
        ],
    )(*kept)


def ring_gather(lay, shard):
    planes = lay.planes
    rows = shard.shape[1]
    if planes > 4:
        piece = lax.all_gather(shard, "dp", axis=1, tiled=True)
        across = lay.route(piece, lambda c, z, t: (c, z, (t + 2) % 4) if c == t // 2 else None)
        return jnp.where(lay.relays, piece, across)
    relay = lambda c, z, t: (c, (z + 1) % planes, t) if c == t // 2 else None
    whole = jnp.zeros((shard.shape[0], planes * rows, shard.shape[2]), shard.dtype)
    piece = shard
    for step in range(planes):
        across = lay.route(piece, lambda c, z, t: (c, z, (t + 2) % 4) if c == t // 2 else None)
        chosen = jnp.where(lay.relays, piece, across)
        whole = lax.dynamic_update_slice(whole, chosen, (0, ((lay.plane - step) % planes) * rows, 0))
        if step + 1 < planes:
            piece = lay.route(piece, relay)
    return whole


def ring_scatter(lay, total, holder):
    planes = lay.planes
    rows = total.shape[1] // planes
    low = total.astype(LOW)
    across = lay.route(
        low, lambda c, z, t: (c, z, (t + 2) % 4) if (c != t // 2 and t % 2 == holder) else None
    )
    summed = low.astype(WIDE) + across.astype(WIDE)
    if planes > 4:
        return lax.psum_scatter(summed.astype(LOW), "dp", scatter_dimension=1, tiled=True)
    relay = lambda c, z, t: (c, (z + 1) % planes, t) if (c == t // 2 and t % 2 == holder) else None
    take = lambda j: lax.dynamic_slice_in_dim(summed, (j % planes) * rows, rows, 1)
    running = take(lay.plane - 1)
    for step in range(1, planes):
        running = lay.route(running.astype(LOW), relay).astype(WIDE) + take(lay.plane - 1 - step)
    return running.astype(LOW)


def hand_back(lay, value, holder, section):
    same = lay.route(
        value[0], lambda c, z, t: (section, z, t) if (c == t // 2 and t % 2 == holder) else None
    )
    beside = lay.route(
        value[1], lambda c, z, t: (section, z, t ^ 1) if (c == t // 2 and t % 2 == holder) else None
    )
    return same.astype(WIDE) + beside.astype(WIDE)


def general_body(block_input, w_self, w_self_out, w_cross, w_up, w_down, norm_gains, lengths, task_mask, out_grad):
    lay = Layout()
    seqs, rows, width = block_input.shape[1:]
    slot = rows * lay.chips
    sec = lay.core
    item = lay.item

    def spread(value, first):
        pick = value[jnp.where(first, lay.chip % 2, 1 - lay.chip % 2)]
        flip = 0 if first else 1
        return lay.route(pick, lambda c, z, t: (t // 2, z, 2 * ((t % 2) ^ flip) + c))

    def merge_rows(mine, theirs):
        low_half = jnp.where(lay.core == 0, mine, theirs)
        high_half = jnp.where(lay.core == 0, theirs, mine)
        return jnp.concatenate([low_half[0], low_half[1], high_half[0], high_half[1]], axis=0)

    first = spread(block_input[0], True)
    second = spread(block_input[0], False)
    mine = jnp.where(item == 0, jnp.stack([first, second]), jnp.stack([second, first]))
    x_rows = merge_rows(mine, lay.other_core(mine)).astype(WIDE)

    picked = out_grad[lay.core]
    even = lay.route(picked, lambda c, z, t: (t // 2, z, 2 * c + 1) if t % 2 == 0 else None)
    odd = lay.route(picked, lambda c, z, t: (t // 2, z, 2 * c + 1) if t % 2 == 1 else None)
    mine = jnp.stack([even, odd])
    cotangent = merge_rows(mine, lay.other_core(mine))

    gains_here = norm_gains[0].astype(WIDE)
    gains = jnp.where(sec == lay.role, gains_here, lay.other_core(norm_gains[0]).astype(WIDE))

    depth = w_self.shape[1]
    wide = w_self.shape[3]
    self_block = pack_heads(
        {"q": w_self[0, :, 0], "k": w_self[0, :, 1], "v": w_self[0, :, 2], "o": w_self_out[0].T}
    )
    feed_block = jnp.concatenate([w_up[0], w_down[0].T], axis=1)
    cross_block = w_cross[0].reshape(depth, 2 * wide)

    def collect(block):
        same = lay.route(block, lambda c, z, t: (t // 2, z, t) if c == t % 2 else None)
        beside = lay.route(block, lambda c, z, t: (t // 2, z, t ^ 1) if c != t % 2 else None)
        return jnp.stack([same, beside])

    def collect_cross(block, section):
        same = lay.route(block, lambda c, z, t: (t // 2, z, t) if (c == section and t % 2 == 1) else None)
        beside = lay.route(block, lambda c, z, t: (t // 2, z, t ^ 1) if (c == section and t % 2 == 0) else None)
        return same, beside

    w_att = ring_gather(lay, collect(self_block))
    w_ffn = ring_gather(lay, collect(feed_block))
    memory_side = collect_cross(cross_block, 0)
    query_side = collect_cross(cross_block, 1)
    w_crs = ring_gather(
        lay,
        jnp.stack(
            [
                pack_heads({"q": q[:, :wide], "k": m[:, :wide], "v": m[:, wide:], "o": q[:, wide:]})
                for m, q in zip(memory_side, query_side)
            ]
        ),
    )
    hidden = w_up.shape[2]
    part = lambda w, name: jnp.concatenate([unpack_heads(w[0], name), unpack_heads(w[1], name)], axis=1)
    att = {n: part(w_att, n) for n in "qkvo"}
    crs = {n: part(w_crs, n) for n in "qkvo"}
    up = jnp.concatenate([w_ffn[0, :, :hidden], w_ffn[1, :, :hidden]], axis=1)
    down_t = jnp.concatenate([w_ffn[0, :, hidden:], w_ffn[1, :, hidden:]], axis=1)

    positions = jnp.arange(slot)
    own_length = jnp.where(lay.is_decoder, lengths[1, item], lengths[0, item])
    self_allowed = (positions[None, :] < own_length) & (
        (positions[None, :] <= positions[:, None]) | jnp.logical_not(lay.is_decoder)
    )
    cross_allowed = jnp.broadcast_to(
        ((positions < lengths[0, item]) & (task_mask[item] == 1))[None], (slot, slot)
    )

    def joined(partial):
        low = partial.astype(LOW)
        return low.astype(WIDE) + lay.other_core(low).astype(WIDE)

    normed0 = layer_norm(x_rows, gains[0]).astype(LOW)
    q, k, v = (mm(normed0, att[n]).astype(LOW) for n in "qkv")
    out_self, lse_self = attend(q, k, v, self_allowed)
    x_mid = x_rows + joined(mm_nt(out_self, att["o"]))
    normed1 = layer_norm(x_mid, gains[1]).astype(LOW)

    pre_enc = mm(normed1, up)
    act_enc, slope_enc = gelu_parts(pre_enc)
    act_enc = act_enc.astype(LOW)
    x_late_enc = x_mid + joined(mm_nt(act_enc, down_t))
    memory_enc = layer_norm(x_late_enc, gains[2]).astype(LOW)
    memory = lay.route(memory_enc, lambda c, z, t: (c, z, t ^ 1) if t % 2 == 0 else None)

    cq = mm(normed1, crs["q"]).astype(LOW)
    ck, cv = (mm(memory, crs[n]).astype(LOW) for n in "kv")
    out_cross, lse_cross = attend(cq, ck, cv, cross_allowed)
    x_late = x_mid + joined(mm_nt(out_cross, crs["o"]))
    normed2 = layer_norm(x_late, gains[2]).astype(LOW)
    pre_dec = mm(normed2, up)
    act_dec, slope_dec = gelu_parts(pre_dec)
    act_dec = act_dec.astype(LOW)
    result_dec = (x_late + joined(mm_nt(act_dec, down_t))).astype(LOW)

    d_out = cotangent.astype(WIDE)
    d_pre = (slope_dec * mm(cotangent, down_t)).astype(LOW)
    d_ffn_dec = jnp.concatenate([mm_tn(normed2, d_pre), mm_tn(cotangent, act_dec)], axis=1)
    d_late_norm, d_gain2_dec = norm_back(x_late, gains[2], joined(mm_nt(d_pre, up)))
    d_late = d_out + d_late_norm
    grad_late = d_late.astype(LOW)
    d_att = mm(grad_late, crs["o"]).astype(LOW)
    d_cq, d_ck, d_cv = attend_back(cq, ck, cv, lse_cross, d_att, cross_allowed)
    d_memory = joined(mm_nt(d_ck, crs["k"]) + mm_nt(d_cv, crs["v"]))
    d_crs = {
        "q": mm_tn(normed1, d_cq),
        "k": mm_tn(memory, d_ck),
        "v": mm_tn(memory, d_cv),
        "o": mm_tn(grad_late, out_cross),
    }
    d_mid_norm, d_gain1_dec = norm_back(x_mid, gains[1], joined(mm_nt(d_cq, crs["q"])))
    d_mid_dec = d_late + d_mid_norm

    d_memory = lay.route(d_memory.astype(LOW), lambda c, z, t: (c, z, t ^ 1) if t % 2 == 1 else None).astype(WIDE)
    d_late_enc, d_gain2_enc = norm_back(x_late_enc, gains[2], d_memory)
    grad_late_enc = d_late_enc.astype(LOW)
    d_pre = (slope_enc * mm(grad_late_enc, down_t)).astype(LOW)
    d_ffn_enc = jnp.concatenate([mm_tn(normed1, d_pre), mm_tn(grad_late_enc, act_enc)], axis=1)
    d_mid_norm, d_gain1_enc = norm_back(x_mid, gains[1], joined(mm_nt(d_pre, up)))
    d_mid_enc = d_late_enc + d_mid_norm

    d_mid = jnp.where(lay.is_decoder, d_mid_dec, d_mid_enc)
    grad_mid = d_mid.astype(LOW)
    d_att = mm(grad_mid, att["o"]).astype(LOW)
    d_q, d_k, d_v = attend_back(q, k, v, lse_self, d_att, self_allowed)
    d_norm = joined(mm_nt(d_q, att["q"]) + mm_nt(d_k, att["k"]) + mm_nt(d_v, att["v"]))
    d_att_w = {
        "q": mm_tn(normed0, d_q),
        "k": mm_tn(normed0, d_k),
        "v": mm_tn(normed0, d_v),
        "o": mm_tn(grad_mid, out_self),
    }
    d_first, d_gain0 = norm_back(x_rows, gains[0], d_norm)
    d_rows = d_mid + d_first

    half = 3 * HEAD

    def blocks(parts):
        return jnp.stack(
            [pack_heads({n: parts[n][:, half * b : half * (b + 1)] for n in parts}) for b in range(2)]
        )

    def feed_blocks(both):
        total = both.shape[1] // 2
        return jnp.stack(
            [
                jnp.concatenate(
                    [both[:, hidden * b : hidden * (b + 1)], both[:, total + hidden * b : total + hidden * (b + 1)]],
                    axis=1,
                )
                for b in range(2)
            ]
        )

    self_total = blocks(d_att_w)
    home_self = hand_back(lay, ring_scatter(lay, self_total, 0), 0, 0) + hand_back(
        lay, ring_scatter(lay, self_total, 1), 1, 1
    )
    home_feed = hand_back(lay, ring_scatter(lay, feed_blocks(d_ffn_enc), 0), 0, 0) + hand_back(
        lay, ring_scatter(lay, feed_blocks(d_ffn_dec), 1), 1, 1
    )
    cross_total = ring_scatter(lay, blocks(d_crs), 1)
    side = lambda names: jnp.stack(
        [jnp.concatenate([unpack_heads(cross_total[b], n) for n in names], axis=1) for b in range(2)]
    )
    home_cross = hand_back(lay, side("kv"), 1, 0) + hand_back(lay, side("qo"), 1, 1)

    g_self = jnp.stack([unpack_heads(home_self, n) for n in "qkv"], axis=1)[None]
    g_self_out = unpack_heads(home_self, "o").T[None]
    g_cross = home_cross.reshape(1, depth, 2, wide)
    g_up = home_feed[:, :hidden][None]
    g_down = home_feed[:, hidden:].T[None]

    gain2 = jnp.where(lay.is_decoder, d_gain2_dec, d_gain2_enc)
    gain1 = jnp.where(lay.is_decoder, d_gain1_dec, d_gain1_enc)
    gain_rows = jnp.stack([d_gain0, gain1, gain2])
    slots = jnp.stack(
        [
            jnp.where((lay.role == r) & (lay.core == 0), gain_rows, 0.0)
            for r in range(2)
        ]
    )
    gain_total = lax.psum(slots, AXES)[sec][None]

    def rows_home(value):
        mine = lax.dynamic_slice_in_dim(value, lay.core * 2 * rows, 2 * rows, 0).reshape(2, rows, width)
        a = lay.route(mine[item], lambda c, z, t: (t % 2, z, 2 * c + t // 2))
        b = lay.route(mine[1 - item], lambda c, z, t: (t % 2, z, 2 * c + 1 - t // 2))
        even = lay.chip % 2 == 0
        return jnp.where(even, jnp.stack([a, b]), jnp.stack([b, a]))[None]

    block_output = rows_home(jnp.where(lay.is_decoder, result_dec, memory_enc))
    input_grad = rows_home(d_rows.astype(LOW)).astype(WIDE)
    return (
        block_output,
        input_grad,
        g_self,
        g_self_out,
        g_cross,
        g_up,
        g_down,
        gain_total[:, :2],
        gain_total[:, 2],
    )


def body(block_input, w_self, w_self_out, w_cross, w_up, w_down, norm_gains, lengths, task_mask, out_grad):
    lay = Layout()
    seqs, rows, width = block_input.shape[1:]
    slot = rows * lay.chips
    sec = lay.core
    item = lay.item

    if lay.planes != 4:
        return general_body(
            block_input, w_self, w_self_out, w_cross, w_up, w_down, norm_gains, lengths, task_mask, out_grad
        )

    depth = w_self.shape[1]
    wide = w_self.shape[3]
    hidden = w_up.shape[2]
    self_block = pack_heads(
        {"q": w_self[0, :, 0], "k": w_self[0, :, 1], "v": w_self[0, :, 2], "o": w_self_out[0].T}
    )
    pair = {"q": w_cross[0, :, 0], "o": w_cross[0, :, 1], "k": w_cross[0, :, 0], "v": w_cross[0, :, 1]}
    pieces = [pair[n][:, HEAD * h : HEAD * (h + 1)] for n, h in ORDER]
    cross_block = jnp.where(
        sec == 1, jnp.concatenate(pieces[:6], axis=1), jnp.concatenate(pieces[6:], axis=1)
    )
    kept = block_call(
        lay.planes,
        slot,
        width,
        hidden,
        depth,
        (self_block, cross_block, w_up[0], w_down[0].T, block_input[0], out_grad, norm_gains[0], lengths, task_mask),
    )[:6]
    block_output, input_grad, g_up, g_down, g_qkv, g_out, g_cross, g_gain, g_last = widen_call(kept)
    return (
        block_output[None],
        input_grad[None],
        jnp.swapaxes(g_qkv, 0, 1)[None],
        g_out[None],
        jnp.swapaxes(g_cross, 0, 1)[None],
        g_up[None],
        g_down.T[None],
        g_gain[None],
        g_last,
    )


def solution(mesh):
    placed = (
        P("section", "dp", "tensor", None),
        P("section", "dp", None, "tensor"),
        P("section", "tensor", "dp"),
        P("section", "dp", None, "tensor"),
        P("section", "dp", "tensor"),
        P("section", "tensor", "dp"),
        P("section", None, None),
        P(None, "dp"),
        P("dp", None),
        P("dp", "tensor", None),
    )
    return jax.shard_map(
        body,
        mesh=mesh,
        in_specs=placed,
        out_specs=(
            P("section", "dp", "tensor", None),
            P("section", "dp", "tensor", None),
            P("section", "dp", None, "tensor"),
            P("section", "tensor", "dp"),
            P("section", "dp", None, "tensor"),
            P("section", "dp", "tensor"),
            P("section", "tensor", "dp"),
            P("section", None, None),
            P("section", None),
        ),
        check_vma=False,
    )
```

profile of v0, /device:TPU:2, one launch (start us, length us, event | category | flops | bytes accessed | tf_op | source)
XLA Modules:
  0.0 325.1 jit_solution(17171631709910234428)
XLA Ops:
  0.6 0.0 copy-start
  0.7 1.0 copy.19
  1.7 1.0 slice_bitcast_fusion
  2.8 0.8 concatenate.11.self_in
  3.6 0.0 copy-done
  3.6 0.3 fusion
  4.0 0.8 maximum_select_fusion.crs_in
  4.8 314.2 %shard_map.169 = (bf16[2,256,768]{2,1,0:T(8,128)(2,1)}, bf16[2,256,768]{2,1,0:T(8,128)(2,1)}, bf16[192,1536]{1,0:T(8,128)(2,1)}, bf16[192,384]{1,0:T(8,128)(2,1)...) custom-call(bf16[192,768]{1,0:T(8,128)(2,1)} %concatenate.11.self_in, ...), custom_call_target="tpu_custom_call" | custom-call | tf_op jit(solution)/shard_map/pallas_call | solution.py:1462
  319.0 4.1 %shard_map.170 = (bf16[2,256,768]{2,1,0:T(8,128)(2,1)}, f32[2,256,768]{2,1,0:T(8,128)}, f32[192,768]{1,0:T(8,128)}, f32[192,768]{1,0:T(8,128)}, f32[3,192,192]{2...) custom-call(bf16[2,256,768]{2,1,0:T(8,128)(2,1)} %get-tuple-element.24.block_i, ...), custom_call_target="tpu_custom_call" | custom-call | tf_op jit(solution)/shard_map/pallas_call | solution.py:1511
  323.1 2.0 copy.22
  (11 shorter events, 0.1 us)
Async XLA Ops:
  0.6 3.0 copy-start
where the time goes:
time: 331 us; the launch traced here: 325 us
  Pallas kernels  318 us (96%)
  local copies, waits for them, and re-layouts  5.29 us (2%)
    pallas_call x1, Pallas kernels, block_call(): pl.pallas_call(functools.partial(block_kernel, planes), out_shape=out_sha...  314 us

commit v1 on v0

--- a/solution.py
+++ b/solution.py
@@ -245,7 +245,7 @@
 
 SUMS = ("ffn", "crs", "att")
 DIRECT = ("att", "up")
-ASIDE = (("up", 0), ("dn", 0))
+ASIDE = (("up", 0), ("up", 1), ("dn", 0))
 
 
 def split_three(value):
@@ -329,7 +329,7 @@
     dw_ffn, dw_crs, dw_att, yb_ffn, yb_crs, yb_att, zb_ffn, zb_crs, zb_att,
     att_v, crs_v, up_v, dn_v, a_v, b_v, o_v, do_v, mid_v, late_v, s_v, g_v, c_v, ta, tb, tc,
     send_v, recv_v, kx, qx, vx, gx, dk_v, dv_v, kt_v, lse_v, gain_v, gain_in_v, gain_buf, out_st, dw_st, sum_st,
-    bias_self, bias_cross,
+    bias_self, bias_cross, res_ffn, res_crs, res_att,
     x_sem, x_sent, y0_sent, c_sem, zw_got, zw_sent, yw_got, yw_sent, side_got, side_sent,
     row_got, row_sent, fwd_sem, cot_got, gain_sem, copy_sem, ex_got, ex_sent, mem_got, mem_sent, mf_got, mf_sent,
     dm_got, dm_sent, df_got, df_sent, y_got, y_sent, z_got, z_sent, home_got, home_sent,
@@ -351,6 +351,7 @@
     yb = {"ffn": yb_ffn, "crs": yb_crs, "att": yb_att}
     zb = {"ffn": zb_ffn, "crs": zb_crs, "att": zb_att}
     home = {"ffn": home_ffn, "crs": home_crs, "att": home_att}
+    res = {"ffn": res_ffn, "crs": res_crs, "att": res_att}
     names = {}
 
     def copying(name, source, goal):
@@ -482,7 +483,7 @@
                     arrive(g, k, b)
                 if k + 1 < planes:
                     ring(g, k + 1, b).start()
-            if over and not (k == 0 and g in DIRECT):
+            if over and not (k == 0 and g in DIRECT) and len(skips) < 2:
                 if skips:
                     pl.when(b != skips[0])(lambda: cross_over(g, k, b).start())
                 else:
@@ -835,7 +836,7 @@
 
     def z_hop(g, k, b):
         i = SUMS.index(g)
-        return push(dw[g].at[k, b], zb[g].at[k, b], z_sent.at[i, k, b], z_got.at[i, k, b], at.above)
+        return push(res[g].at[b], zb[g].at[k, b], z_sent.at[i, k, b], z_got.at[i, k, b], at.above)
 
     def leave(g, k):
         @pl.when(other)
@@ -867,7 +868,7 @@
     def home_copy(g, b, section):
         i = SUMS.index(g)
         columns = dw[g].shape[3]
-        source = dw[g].at[planes - 1, b]
+        source = res[g].at[b]
         if g == "crs":
             source = source.at[:, pl.ds((1 - section) * (columns // 2), columns // 2)]
         device = (section, z, 2 * y + b)
@@ -897,6 +898,7 @@
             def _():
                 z_hop(g, before, b).wait_recv()
                 fetch(2, zb[g].at[before, b]).start()
+                z_hop(g, before, b).wait_send()
                 fetch(2, zb[g].at[before, b]).wait()
 
             fetch(0, dw[g].at[k, b]).wait()
@@ -907,12 +909,9 @@
                 q = strip(m, share)
                 total = sum_st[0, q, 0:columns].astype(WIDE) + sum_st[1, q, 0:columns].astype(WIDE)
                 total = total + jnp.where(k > 0, sum_st[2, q, 0:columns].astype(WIDE), 0.0)
-                sum_st[0, q, 0:columns] = total.astype(LOW)
+                res[g][b, q, :] = total.astype(LOW)
 
             each(4, add_rows)
-            back = pltpu.make_async_copy(sum_st.at[0, :, 0:columns], dw[g].at[k, b], sum_sem.at[0])
-            back.start()
-            back.wait()
 
             @pl.when(k + 1 < planes)
             def _():
@@ -1177,6 +1176,8 @@
         exchange(5, i).start()
 
     each(2, far_rows)
+    pl.when(at.encodes)(lambda: sums("ffn", 4, 2))
+    pl.when(at.decodes)(lambda: sums("crs", 2, 2))
     turn(s_v, ta)
     x_in_v = copying("x", x_k, s_v)
     x_in_v.start()
@@ -1194,8 +1195,7 @@
         each(2, att_half)
 
     emit("att", att_block)
-    pl.when(at.encodes)(lambda: sums("ffn", 4, 2))
-    pl.when(at.decodes)(lambda: sums("crs", 2, 2))
+    pl.when(at.decodes)(lambda: sums("crs", 4, 2))
     x_in_v.wait()
 
     def near_rows(n):
@@ -1215,8 +1215,11 @@
     def grad_home(k):
         return k, grad_k.at[strip(k, rows), :], grad_low, gr_sent, gr_got
 
-    for k in range(2):
-        go_home(*grad_home(k))
+    def rows_leave():
+        for k in range(2):
+            go_home(*grad_home(k))
+
+    pl.when(relay)(rows_leave)
 
     def gain_hop(n, source, device):
         return push(source, gain_buf.at[n], gr_hop_sent.at[n], gr_hop_got.at[n], device)
@@ -1273,8 +1276,13 @@
     def y3_home(k):
         return k, y3_k.at[strip(k, rows), :], block_out, blk_sent, blk_got
 
+    def out_leaves():
+        for k in range(2):
+            go_home(*y3_home(k))
+
     @pl.when(at.decodes)
     def _():
+        sums("att", 0, 2)
         copies = [copying("act", act_k, a_v), copying("late", late_k, mid_v)]
         for copy in copies:
             copy.start()
@@ -1304,16 +1312,26 @@
         y3_put = copying("out", out_st, y3_k)
         y3_put.start()
         y3_put.wait()
-        for k in range(2):
-            go_home(*y3_home(k))
+        pl.when(relay)(out_leaves)
+
+    @pl.when(other)
+    def _():
+        for k in range(planes):
+            for b in range(2):
+                y_hop("att", k, b).wait_send()
+        rows_leave()
+        pl.when(at.decodes)(out_leaves)
 
     pl.when(at.encodes)(lambda: sums("ffn", 6, 2))
-    pl.when(at.decodes)(lambda: sums("crs", 4, 4))
+    pl.when(at.decodes)(lambda: sums("crs", 6, 2))
 
     def last_sums(n):
-        sum_at("att", n)
+        @pl.when(jnp.logical_or(at.encodes, n >= 2))
+        def _():
+            sum_at("att", n)
+
         for m in range(planes):
-            pl.when(n == m)(functools.partial(gain_step, m))
+            pl.when(n == 2 * m + 1)(functools.partial(gain_step, m))
 
     each(2 * planes, last_sums)
 
@@ -1355,17 +1373,17 @@
     for g in SUMS:
         there = at.decodes if g == "crs" else jnp.logical_or(at.decodes, at.encodes)
 
-        @pl.when(both(other, there))
-        def _():
-            for k in range(planes):
-                for b in range(2):
-                    y_hop(g, k, b).wait_send()
+        if g != "att":
+
+            @pl.when(both(other, there))
+            def _():
+                for k in range(planes):
+                    for b in range(2):
+                        y_hop(g, k, b).wait_send()
 
         @pl.when(both(relay, there))
         def _():
             for b in range(2):
-                for k in range(planes - 1):
-                    z_hop(g, k, b).wait_send()
                 for section in sections(g):
                     keeps, source, copy = home_copy(g, b, section)
 
@@ -1446,6 +1464,7 @@
         + [v((planes + 6, 8, width), WIDE)]
         + [v((2 * rows, width), LOW), v((2, 2, depth, 2 * hidden), LOW), v((3, depth, 2 * hidden), LOW)]
         + [v((slot, TILE), LOW)] * 2
+        + [v((2, depth, wides[g]), LOW) for g in SUMS]
         + [dma((groups, 2)), dma((groups,)), dma((groups,)), dma((2, 2))]
         + [dma((groups, planes, 2))] * 4
         + [dma((groups, 2))] * 2
@@ -1489,10 +1508,10 @@
     each(4, strips)
     tiles = [crs_in[:, TILE * n : TILE * (n + 1)].astype(WIDE) for n in range(3)]
     mixed = jnp.where(c == 1, tiles[1], tiles[2])
-    crs_out[0, :, 0:TILE] = tiles[0]
-    crs_out[0, :, TILE : TILE + HEAD] = mixed[:, 0:HEAD]
-    crs_out[1, :, 0:TILE] = jnp.where(c == 1, tiles[2], tiles[1])
-    crs_out[1, :, TILE : TILE + HEAD] = pltpu.roll(mixed, HEAD, 1)[:, 0:HEAD]
+    crs_out[:, 0, 0:TILE] = tiles[0]
+    crs_out[:, 0, TILE : TILE + HEAD] = mixed[:, 0:HEAD]
+    crs_out[:, 1, 0:TILE] = jnp.where(c == 1, tiles[2], tiles[1])
+    crs_out[:, 1, TILE : TILE + HEAD] = pltpu.roll(mixed, HEAD, 1)[:, 0:HEAD]
     q_tile, q_o, o_tile, k_tile, v_tile, k_v = (att_in[:, TILE * n : TILE * (n + 1)].astype(WIDE) for n in range(6))
     for n, (whole, rest) in enumerate(((q_tile, q_o), (k_tile, k_v), (v_tile, pltpu.roll(k_v, HEAD, 1)))):
         qkv_out[n, :, 0:TILE] = whole
@@ -1513,7 +1532,7 @@
         out_shape=[
             shape((2, rows, width), LOW), shape((2, rows, width), WIDE), shape((depth, hidden), WIDE),
             shape((depth, hidden), WIDE), shape((3, depth, wide), WIDE), shape((wide, depth), WIDE),
-            shape((2, depth, wide), WIDE), shape((2, width), WIDE), shape((1, width), WIDE),
+            shape((depth, 2, wide), WIDE), shape((2, width), WIDE), shape((1, width), WIDE),
         ],
     )(*kept)
 
@@ -1818,7 +1837,7 @@
         input_grad[None],
         jnp.swapaxes(g_qkv, 0, 1)[None],
         g_out[None],
-        jnp.swapaxes(g_cross, 0, 1)[None],
+        g_cross[None],
         g_up[None],
         g_down.T[None],
         g_gain[None],

time: 331 us -> 314 us (0.949); the launches traced: 325 us -> 313 us
  Pallas kernels: 318 us -> 308 us
    pallas_call x1, Pallas kernels: 314 us -> 304 us  [block_call(): pl.pallas_call(functools.partial(block_kernel, planes), out_shape=out_sha...]
where the time goes in v1:
time: 314 us; the launch traced here: 313 us
  Pallas kernels  308 us (98%)
  local copies, waits for them, and re-layouts  3.24 us (1%)
    pallas_call x1, Pallas kernels, block_call(): pl.pallas_call(functools.partial(block_kernel, planes), out_shape=out_sha...  304 us

profile of v1, /device:TPU:2, one launch (start us, length us, event | category | flops | bytes accessed | tf_op | source)
XLA Modules:
  0.0 312.8 jit_solution(1459174297234084752)
XLA Ops:
  0.6 0.0 copy-start
  0.7 1.0 copy.19
  1.7 1.0 slice_bitcast_fusion
  2.8 0.8 concatenate.11.self_in
  3.6 0.0 copy-done
  3.6 0.3 fusion
  4.0 0.8 maximum_select_fusion.crs_in
  4.8 303.9 %shard_map.169 = (bf16[2,256,768]{2,1,0:T(8,128)(2,1)}, bf16[2,256,768]{2,1,0:T(8,128)(2,1)}, bf16[192,1536]{1,0:T(8,128)(2,1)}, bf16[192,384]{1,0:T(8,128)(2,1)...) custom-call(bf16[192,768]{1,0:T(8,128)(2,1)} %concatenate.11.self_in, ...), custom_call_target="tpu_custom_call" | custom-call | tf_op jit(solution)/shard_map/pallas_call | solution.py:1481
  308.7 4.1 %shard_map.170 = (bf16[2,256,768]{2,1,0:T(8,128)(2,1)}, f32[2,256,768]{2,1,0:T(8,128)}, f32[192,768]{1,0:T(8,128)}, f32[192,768]{1,0:T(8,128)}, f32[3,192,192]{2...) custom-call(bf16[2,256,768]{2,1,0:T(8,128)(2,1)} %get-tuple-element.24.block_i, ...), custom_call_target="tpu_custom_call" | custom-call | tf_op jit(solution)/shard_map/pallas_call | solution.py:1530
  (11 shorter events, 0.1 us)
Async XLA Ops:
  0.6 3.0 copy-start

commit v2 on v1

--- a/solution.py
+++ b/solution.py
@@ -326,14 +326,14 @@
     planes, self_in, crs_in, up_in, dn_in, x_in, cot_in, gain_in, lengths, task_mask,
     block_out, grad_low, home_ffn, home_crs, home_att, gain_out,
     cot, first_k, x_k, second_k, late_k, memory_k, p_k, o_k, lse_k, pc_k, oc_k, lsec_k, act_k, grad_k, y3_k,
-    dw_ffn, dw_crs, dw_att, yb_ffn, yb_crs, yb_att, zb_ffn, zb_crs, zb_att,
+    dw_ffn, dw_crs, dw_att, yb_ffn, yb_crs, yb_att, zb_ffn, zb_crs, zb_att, via_att,
     att_v, crs_v, up_v, dn_v, a_v, b_v, o_v, do_v, mid_v, late_v, s_v, g_v, c_v, ta, tb, tc,
     send_v, recv_v, kx, qx, vx, gx, dk_v, dv_v, kt_v, lse_v, gain_v, gain_in_v, gain_buf, out_st, dw_st, sum_st,
     bias_self, bias_cross, res_ffn, res_crs, res_att,
     x_sem, x_sent, y0_sent, c_sem, zw_got, zw_sent, yw_got, yw_sent, side_got, side_sent,
     row_got, row_sent, fwd_sem, cot_got, gain_sem, copy_sem, ex_got, ex_sent, mem_got, mem_sent, mf_got, mf_sent,
     dm_got, dm_sent, df_got, df_sent, y_got, y_sent, z_got, z_sent, home_got, home_sent,
-    blk_got, blk_sent, gr_got, gr_sent, gr_hop_got, gr_hop_sent, sum_sem, dw_sem,
+    blk_got, blk_sent, gr_got, gr_sent, gr_hop_got, gr_hop_sent, sum_sem, dw_sem, via_got, via_sent, hand_got, hand_sent,
 ):
     at = Place(planes)
     c, z, t, y, r = at.c, at.z, at.t, at.y, at.r
@@ -838,11 +838,22 @@
         i = SUMS.index(g)
         return push(res[g].at[b], zb[g].at[k, b], z_sent.at[i, k, b], z_got.at[i, k, b], at.above)
 
+    def via_hop(k):
+        diagonal = (c, z, lax.rem(t + 2, 4) + 1 - 2 * r)
+        return push(dw_att.at[k, 1], via_att.at[k], via_sent.at[k], via_got.at[k], diagonal)
+
+    def hand_on(k):
+        return push(via_att.at[k], yb_att.at[k, 1], hand_sent.at[k], hand_got.at[k], at.beside)
+
     def leave(g, k):
         @pl.when(other)
         def _():
-            for b in range(2):
-                y_hop(g, k, b).start()
+            y_hop(g, k, 0).start()
+            if g == "att":
+                pl.when(at.decodes)(lambda: y_hop(g, k, 1).start())
+                pl.when(at.encodes)(lambda: via_hop(k).start())
+            else:
+                y_hop(g, k, 1).start()
 
     def emit(g, compute):
         columns = dw[g].shape[3]
@@ -890,7 +901,12 @@
         @jax.named_scope("sum_" + g)
         def _():
             before = lax.max(k - 1, 0)
-            y_hop(g, k, b).wait_recv()
+            if g == "att":
+                detour = both(at.encodes, b == 1)
+                pl.when(detour)(lambda: hand_on(k).wait_recv())
+                pl.when(jnp.logical_not(detour))(lambda: y_hop(g, k, b).wait_recv())
+            else:
+                y_hop(g, k, b).wait_recv()
             fetch(0, dw[g].at[k, b]).start()
             fetch(1, yb[g].at[k, b]).start()
 
@@ -950,6 +966,8 @@
 
     @pl.when(at.encodes)
     def _():
+        turn(s_v, ta)
+
         def back_rows(m):
             n = lax.div(m, 2)
             own = lax.rem(m, 2) == 0
@@ -985,7 +1003,7 @@
 
         each(tiles, back_rows)
 
-    turn(s_v, ta)
+    pl.when(at.decodes)(lambda: turn(s_v, ta))
     turn(c_v, tb)
 
     def ffn_block(s, j):
@@ -1146,9 +1164,9 @@
         each(6, self_head)
 
     def enc_hook(n):
-        @pl.when(jnp.logical_and(n != 0, n != 3))
-        def _():
-            sum_at("ffn", n - 1 - lax.div(n, 4))
+        @pl.when(jnp.logical_and(n != 2, n != 5))
+        def _():
+            sum_at("ffn", n - lax.div(n, 3))
 
     def dec_hook(n):
         @pl.when(n < 4)
@@ -1282,6 +1300,13 @@
 
     @pl.when(at.decodes)
     def _():
+        @pl.when(relay)
+        @jax.named_scope("hand_on")
+        def _():
+            for k in range(planes):
+                via_hop(k).wait_recv()
+                hand_on(k).start()
+
         sums("att", 0, 2)
         copies = [copying("act", act_k, a_v), copying("late", late_k, mid_v)]
         for copy in copies:
@@ -1317,8 +1342,9 @@
     @pl.when(other)
     def _():
         for k in range(planes):
-            for b in range(2):
-                y_hop("att", k, b).wait_send()
+            y_hop("att", k, 0).wait_send()
+            pl.when(at.decodes)(lambda: y_hop("att", k, 1).wait_send())
+            pl.when(at.encodes)(lambda: via_hop(k).wait_send())
         rows_leave()
         pl.when(at.decodes)(out_leaves)
 
@@ -1331,7 +1357,7 @@
             sum_at("att", n)
 
         for m in range(planes):
-            pl.when(n == 2 * m + 1)(functools.partial(gain_step, m))
+            pl.when(n == 2 * m)(functools.partial(gain_step, m))
 
     each(2 * planes, last_sums)
 
@@ -1390,6 +1416,11 @@
                     @pl.when(jnp.logical_not(keeps))
                     def _():
                         copy.wait_send()
+
+    @pl.when(both(relay, at.decodes))
+    def _():
+        for k in range(planes):
+            hand_on(k).wait_send()
 
     gain_copy.wait_send()
     for g in DIRECT:
@@ -1445,6 +1476,7 @@
         + [shape(acts, LOW)]
         + [shape((2 * rows, width), LOW)] * 2
         + [shape((planes, 2, depth, wides[g]), LOW) for g in SUMS] * 3
+        + [shape((planes, depth, width), LOW)]
     )
     dma = pltpu.SemaphoreType.DMA
     v = pltpu.VMEM
@@ -1475,6 +1507,7 @@
         + [dma((2,))] * 4
         + [dma((planes + 6,))] * 2
         + [dma((3,)), dma((2,))]
+        + [dma((planes,))] * 4
     )
     any_spec = pl.BlockSpec(memory_space=pl.ANY)
     vmem_spec = pl.BlockSpec(memory_space=pltpu.VMEM)

time: 314 us -> 309 us (0.984)
  Pallas kernels: 308 us -> 302 us
    pallas_call x1, Pallas kernels: 304 us -> 298 us  [block_call(): pl.pallas_call(functools.partial(block_kernel, planes), out_shape=out_sha...]
where the time goes in v2:
time: 309 us; the launch traced here: 307 us
  Pallas kernels  302 us (98%)
  local copies, waits for them, and re-layouts  3.24 us (1%)
    pallas_call x1, Pallas kernels, block_call(): pl.pallas_call(functools.partial(block_kernel, planes), out_shape=out_sha...  298 us

profile of v2, /device:TPU:2, one launch (start us, length us, event | category | flops | bytes accessed | tf_op | source)
XLA Modules:
  0.0 307.1 jit_solution(7916993622487361772)
XLA Ops:
  0.6 0.0 copy-start
  0.7 1.0 copy.19
  1.7 1.0 slice_bitcast_fusion
  2.8 0.8 concatenate.11.self_in
  3.6 0.0 copy-done
  3.6 0.3 fusion
  4.0 0.8 maximum_select_fusion.crs_in
  4.8 298.2 %shard_map.169 = (bf16[2,256,768]{2,1,0:T(8,128)(2,1)}, bf16[2,256,768]{2,1,0:T(8,128)(2,1)}, bf16[192,1536]{1,0:T(8,128)(2,1)}, bf16[192,384]{1,0:T(8,128)(2,1)...) custom-call(bf16[192,768]{1,0:T(8,128)(2,1)} %concatenate.11.self_in, ...), custom_call_target="tpu_custom_call" | custom-call | tf_op jit(solution)/shard_map/pallas_call | solution.py:1514
  303.0 4.1 %shard_map.170 = (bf16[2,256,768]{2,1,0:T(8,128)(2,1)}, f32[2,256,768]{2,1,0:T(8,128)}, f32[192,768]{1,0:T(8,128)}, f32[192,768]{1,0:T(8,128)}, f32[3,192,192]{2...) custom-call(bf16[2,256,768]{2,1,0:T(8,128)(2,1)} %get-tuple-element.24.block_i, ...), custom_call_target="tpu_custom_call" | custom-call | tf_op jit(solution)/shard_map/pallas_call | solution.py:1563
  (11 shorter events, 0.1 us)
Async XLA Ops:
  0.6 3.0 copy-start

commit v3 on v2

--- a/solution.py
+++ b/solution.py
@@ -1214,6 +1214,14 @@
 
     emit("att", att_block)
     pl.when(at.decodes)(lambda: sums("crs", 4, 2))
+
+    @pl.when(both(relay, at.decodes))
+    @jax.named_scope("hand_on")
+    def _():
+        for k in range(planes):
+            via_hop(k).wait_recv()
+            hand_on(k).start()
+
     x_in_v.wait()
 
     def near_rows(n):
@@ -1300,13 +1308,6 @@
 
     @pl.when(at.decodes)
     def _():
-        @pl.when(relay)
-        @jax.named_scope("hand_on")
-        def _():
-            for k in range(planes):
-                via_hop(k).wait_recv()
-                hand_on(k).start()
-
         sums("att", 0, 2)
         copies = [copying("act", act_k, a_v), copying("late", late_k, mid_v)]
         for copy in copies:
@@ -1348,13 +1349,17 @@
         rows_leave()
         pl.when(at.decodes)(out_leaves)
 
-    pl.when(at.encodes)(lambda: sums("ffn", 6, 2))
+    @pl.when(at.encodes)
+    def _():
+        sums("att", 1, 1)
+        sums("ffn", 6, 2)
+
     pl.when(at.decodes)(lambda: sums("crs", 6, 2))
 
     def last_sums(n):
-        @pl.when(jnp.logical_or(at.encodes, n >= 2))
-        def _():
-            sum_at("att", n)
+        @pl.when(jnp.logical_or(both(at.encodes, n >= 1), n >= 2))
+        def _():
+            sum_at("att", n + jnp.where(at.encodes, 1 - 2 * lax.rem(n, 2), 0))
 
         for m in range(planes):
             pl.when(n == 2 * m)(functools.partial(gain_step, m))

time: 309 us -> 307 us (level)
  Pallas kernels: 302 us -> 298 us
    pallas_call x1, Pallas kernels: 298 us -> 294 us  [block_call(): pl.pallas_call(functools.partial(block_kernel, planes), out_shape=out_sha...]
where the time goes in v3:
time: 307 us; the launch traced here: 303 us
  Pallas kernels  298 us (97%)
  local copies, waits for them, and re-layouts  3.24 us (1%)
    pallas_call x1, Pallas kernels, block_call(): pl.pallas_call(functools.partial(block_kernel, planes), out_shape=out_sha...  294 us

profile of v3, /device:TPU:2, one launch (start us, length us, event | category | flops | bytes accessed | tf_op | source)
XLA Modules:
  0.0 303.2 jit_solution(16403271107728601458)
XLA Ops:
  0.6 0.0 copy-start
  0.7 1.0 copy.19
  1.7 1.0 slice_bitcast_fusion
  2.8 0.8 concatenate.11.self_in
  3.6 0.0 copy-done
  3.6 0.3 fusion
  4.0 0.8 maximum_select_fusion.crs_in
  4.8 294.3 %shard_map.169 = (bf16[2,256,768]{2,1,0:T(8,128)(2,1)}, bf16[2,256,768]{2,1,0:T(8,128)(2,1)}, bf16[192,1536]{1,0:T(8,128)(2,1)}, bf16[192,384]{1,0:T(8,128)(2,1)...) custom-call(bf16[192,768]{1,0:T(8,128)(2,1)} %concatenate.11.self_in, ...), custom_call_target="tpu_custom_call" | custom-call | tf_op jit(solution)/shard_map/pallas_call | solution.py:1519
  299.1 4.1 %shard_map.170 = (bf16[2,256,768]{2,1,0:T(8,128)(2,1)}, f32[2,256,768]{2,1,0:T(8,128)}, f32[192,768]{1,0:T(8,128)}, f32[192,768]{1,0:T(8,128)}, f32[3,192,192]{2...) custom-call(bf16[2,256,768]{2,1,0:T(8,128)(2,1)} %get-tuple-element.24.block_i, ...), custom_call_target="tpu_custom_call" | custom-call | tf_op jit(solution)/shard_map/pallas_call | solution.py:1568
  (11 shorter events, 0.1 us)
Async XLA Ops:
  0.6 3.0 copy-start

commit v4 on v3

--- a/solution.py
+++ b/solution.py
@@ -245,7 +245,7 @@
 
 SUMS = ("ffn", "crs", "att")
 DIRECT = ("att", "up")
-ASIDE = (("up", 0), ("up", 1), ("dn", 0))
+ASIDE = (("up", 0), ("up", 1), ("dn", 0), ("dn", 1))
 
 
 def split_three(value):

time: 307 us -> 307 us (level)
  no operation moved by 1% of the time
where the time goes in v4:
time: 307 us; the launch traced here: 304 us
  Pallas kernels  299 us (97%)
  local copies, waits for them, and re-layouts  3.24 us (1%)
    pallas_call x1, Pallas kernels, block_call(): pl.pallas_call(functools.partial(block_kernel, planes), out_shape=out_sha...  295 us

profile of v4, /device:TPU:2, one launch (start us, length us, event | category | flops | bytes accessed | tf_op | source)
XLA Modules:
  0.0 304.1 jit_solution(13990276044045965456)
XLA Ops:
  0.6 0.0 copy-start
  0.7 1.0 copy.19
  1.7 1.0 slice_bitcast_fusion
  2.8 0.8 concatenate.11.self_in
  3.6 0.0 copy-done
  3.6 0.3 fusion
  4.0 0.8 maximum_select_fusion.crs_in
  4.8 295.2 %shard_map.169 = (bf16[2,256,768]{2,1,0:T(8,128)(2,1)}, bf16[2,256,768]{2,1,0:T(8,128)(2,1)}, bf16[192,1536]{1,0:T(8,128)(2,1)}, bf16[192,384]{1,0:T(8,128)(2,1)...) custom-call(bf16[192,768]{1,0:T(8,128)(2,1)} %concatenate.11.self_in, ...), custom_call_target="tpu_custom_call" | custom-call | tf_op jit(solution)/shard_map/pallas_call | solution.py:1519
  300.0 4.1 %shard_map.170 = (bf16[2,256,768]{2,1,0:T(8,128)(2,1)}, f32[2,256,768]{2,1,0:T(8,128)}, f32[192,768]{1,0:T(8,128)}, f32[192,768]{1,0:T(8,128)}, f32[3,192,192]{2...) custom-call(bf16[2,256,768]{2,1,0:T(8,128)(2,1)} %get-tuple-element.24.block_i, ...), custom_call_target="tpu_custom_call" | custom-call | tf_op jit(solution)/shard_map/pallas_call | solution.py:1568
  (11 shorter events, 0.1 us)
Async XLA Ops:
  0.6 3.0 copy-start
